TPU v7x, 128 devices: a whole 4x4x4 slice. The times are simulated.
128 devices in a mesh: region: 8 (over y, core), slab: 16 (over x, z).
Axes of the slice: x: 4, y: 4, z: 4, core: 2. Of those that a mesh axis runs over, the one named last changes fastest.
Arguments:
- coarse: float32 [32, 176, 8, 256], P('region', 'slab'), may hold values from -6 to 6
- cover: int32 [8, 16, 16, 3], replicated, may hold values from 0 to 175, as said below
- sizes: int32 [8, 2], replicated, may hold values from 6 to 16, as said below
- tclass: int32 [8, 48, 192], P('region'), may hold values from 0 to 15
- up_rows: float32 [384, 128], replicated, may hold values from -0.5 to 0.5
- up_cols: float32 [128, 1536], replicated, may hold values from -0.5 to 0.5
- lift: float32 [32, 64], replicated, may hold values from -1 to 1
- kernel_one: bfloat16 [3, 3, 64, 64], replicated, may hold values from -0.25 to 0.25
- kernel_two: bfloat16 [3, 3, 64, 64], replicated, may hold values from -0.25 to 0.25
- gain_table: float32 [16, 64], replicated, may hold values from 0.1 to 1.9
- shift_table: float32 [16, 64], replicated, may hold values from -3 to 3
Outputs:
- fine_out: bfloat16 [8, 384, 98304], P('region', 'slab')
Inputs may be any that keep to these rules, and one draw needn't show every extreme that they name: `cover`: for each region r there is an anchor (g, h) such that entry (r, i, j) names global block row g + i and block column (h + j) % 176 (longitude wraps around), as owner (g + i) // 4, row (g + i) % 4 and that column. `sizes`: column 0 lies in 6 to 16, column 1 in 6 to 16; in every draw one region has both full and another has both least.
All inputs are finite; a program needn't handle non-finite values.
Results may differ from a plain program's by a relative error of at most 0.0053.
Values may be sent and summed in bfloat16 or wider, within the bound.
A program may use at most 192 MiB of HBM per device.

v0:
```python
import jax
import jax.numpy as jnp
from jax import lax
from jax.sharding import PartitionSpec as P


def extended(cells, sides, width):
    for axis, dim in sides:
        count = lax.axis_size(axis)
        ends = count - 1
        head = lax.slice_in_dim(cells, 0, width, axis=dim)
        tail = lax.slice_in_dim(cells, cells.shape[dim] - width, cells.shape[dim], axis=dim)
        cells = jnp.concatenate(
            [
                lax.ppermute(tail, axis, [(i, (i + 1) % count) for i in range(ends)]),
                cells,
                lax.ppermute(head, axis, [((i + 1) % count, i) for i in range(ends)]),
            ],
            axis=dim,
        )
    return cells


def pair_kernel(kernel):
    channels = kernel.shape[2]
    empty_block = jnp.zeros((3, channels, channels), kernel.dtype)
    groups = []
    for offset in (-1, 0, 1):
        rows_in = []
        for side_in in (0, 1):
            cols_out = []
            for side_out in (0, 1):
                column = 2 * offset + side_in - side_out + 1
                if 0 <= column <= 2:
                    cols_out.append(kernel[:, column])
                else:
                    cols_out.append(empty_block)
            rows_in.append(jnp.concatenate(cols_out, axis=2))
        groups.append(jnp.concatenate(rows_in, axis=1))
    return jnp.concatenate(groups, axis=1)


def conv_pairs(padded, weights, out_rows):
    pair_count = padded.shape[1]
    zero_edge = jnp.zeros((padded.shape[0], 1, padded.shape[2]), padded.dtype)
    widened = jnp.concatenate([zero_edge, padded, zero_edge], axis=1)
    stacked = jnp.concatenate(
        [widened[:, 0:pair_count], widened[:, 1 : pair_count + 1], widened[:, 2 : pair_count + 2]],
        axis=2,
    )
    summed = None
    for shift_row in range(3):
        partial_value = jnp.einsum(
            "ypk,kn->ypn",
            stacked[shift_row : shift_row + out_rows],
            weights[shift_row],
            preferred_element_type=jnp.float32,
        )
        summed = partial_value if summed is None else summed + partial_value
    return summed


def local(
    coarse,
    cover,
    sizes,
    tclass,
    up_rows,
    up_cols,
    lift,
    kernel_one,
    kernel_two,
    gain_table,
    shift_table,
):
    band = lax.all_gather(coarse, "slab", axis=1, tiled=True)
    n_slab = lax.axis_size("slab")
    owner = lax.axis_index("region")
    slab_index = lax.axis_index("slab")
    block_rows = cover.shape[1]
    block_cols = cover.shape[2]
    block_height = band.shape[2]
    block_span = band.shape[3]
    in_channels = lift.shape[0]
    channels = lift.shape[1]
    fine_rows = up_rows.shape[0]
    fine_cols = up_cols.shape[1]
    rows_dev = fine_rows // n_slab
    pair_count = fine_cols // 2
    col_share = block_cols // n_slab
    rows_full = up_rows.reshape(fine_rows, block_rows, block_height)
    covered = cover
    covered = lax.dynamic_slice_in_dim(covered, slab_index * col_share, col_share, 2)
    blocks = band[covered[..., 1], covered[..., 2]]
    mine = covered[..., 0] == owner
    blocks = jnp.where(mine[..., None, None], blocks, 0.0)
    partial_cols = lax.psum_scatter(
        jnp.einsum(
            "ykb,rkjbw->ryjw",
            rows_full,
            blocks,
            precision=lax.Precision.HIGHEST,
            preferred_element_type=jnp.float32,
        ),
        "region",
        scatter_dimension=0,
        tiled=True,
    )
    partial_rows = lax.all_to_all(partial_cols, "slab", split_axis=1, concat_axis=2, tiled=True)
    partial_rows = partial_rows[0].reshape(
        rows_dev, block_cols, block_span // in_channels, in_channels
    )
    cols_op = up_cols.reshape(block_cols, block_span // in_channels, fine_cols)
    upsampled = jnp.einsum("ykwc,kwx->ycx", partial_rows, cols_op, precision=lax.Precision.HIGHEST)
    lifted = jnp.einsum("ycx,cd->yxd", upsampled, lift, precision=lax.Precision.HIGHEST)
    lifted = lifted.reshape(rows_dev, pair_count, 2 * channels)
    region_size = sizes[owner]
    valid_rows = region_size[0] * (fine_rows // block_rows)
    valid_cols = region_size[1] * (fine_cols // block_cols)
    col_index = (
        2 * jnp.arange(pair_count, dtype=jnp.int32)[:, None]
        + jnp.arange(2 * channels, dtype=jnp.int32)[None, :] // channels
    )
    col_valid = col_index < valid_cols

    def row_valid(first_row, row_count):
        global_rows = first_row + jnp.arange(row_count, dtype=jnp.int32)
        return (global_rows, (global_rows >= 0) & (global_rows < valid_rows))

    own_rows, own_valid = row_valid(slab_index * rows_dev, rows_dev)
    inside = own_valid[:, None, None] & col_valid[None]
    fine_in = jnp.where(inside, lifted, 0.0).astype(jnp.bfloat16)
    activated = jax.nn.silu(fine_in.astype(jnp.float32)).astype(jnp.bfloat16)
    tile_count = tclass.shape[1]
    tile_cols = tclass.shape[2]
    tile_rows = fine_rows // tile_count
    class_ids = jnp.arange(gain_table.shape[0], dtype=jnp.int32)
    weights_one = pair_kernel(kernel_one)
    weights_two = pair_kernel(kernel_two)
    padded = extended(activated, (("slab", 0),), 1)
    first_conv = conv_pairs(padded, weights_one, rows_dev)
    row_count = first_conv.shape[0]
    global_rows, valid = row_valid(slab_index * rows_dev, row_count)
    tile_index = jnp.clip(global_rows // tile_rows, 0, tile_count - 1)
    row_classes = tclass[0][tile_index]
    onehot = (row_classes[..., None] == class_ids[None, None, :]).astype(jnp.float32)
    gain_rows = jnp.einsum("rtk,kc->rtc", onehot, gain_table, precision=lax.Precision.HIGHEST)
    shift_rows = jnp.einsum("rtk,kc->rtc", onehot, shift_table, precision=lax.Precision.HIGHEST)
    gain_rows = jnp.concatenate([gain_rows, gain_rows], axis=-1)
    shift_rows = jnp.concatenate([shift_rows, shift_rows], axis=-1)
    shaped = first_conv.reshape(row_count, tile_cols, pair_count // tile_cols, 2 * channels)
    modulated = shaped * gain_rows[:, :, None, :] + shift_rows[:, :, None, :]
    modulated = modulated.reshape(row_count, pair_count, 2 * channels)
    retain = valid[:, None, None] & col_valid[None]
    hidden = jnp.where(retain, jax.nn.silu(modulated), 0.0).astype(jnp.bfloat16)
    padded_hidden = extended(hidden, (("slab", 0),), 1)
    second_conv = conv_pairs(padded_hidden, weights_two, rows_dev)
    result = jnp.where(inside, fine_in.astype(jnp.float32) + second_conv, 0.0).astype(jnp.bfloat16)
    return result.reshape(1, rows_dev, pair_count * 2 * channels)


def solution(mesh):
    return jax.shard_map(
        local,
        mesh=mesh,
        in_specs=(
            P("region", "slab", None, None),
            P(),
            P(),
            P("region", None, None),
            P(),
            P(),
            P(),
            P(),
            P(),
            P(),
            P(),
        ),
        out_specs=P("region", "slab", None),
        check_vma=False,
    )
```

profile of v0, /device:TPU:0, one launch (start us, length us, event | category | flops | bytes accessed | tf_op | source)
XLA Modules:
  0.0 312.1 jit_solution(15487417491095555489)
XLA Ops:
  9.9 60.9 %all-gather.2.cloned.1.call-done = f32[4,176,8,256]{3,2,1,0:T(8,128)} async-done(((f32[4,11,8,256]{3,2,1,0:T(8,128)}), f32[4,176,8,256]{3,2,1,0:T(8,128)}) %all-gather.2.cloned.1.call-update) | async-done | bytes 5767184 | tf_op jit(solution)/shard_map/all_gather | solution.py:76
  70.8 3.5 %gather_fusion = f32[128,8,256]{2,1,0:T(8,128)S(1)} fusion(f32[4,176,8,256]{3,2,1,0:T(8,128)} %all-gather.2.cloned.1.call-done, s32[128]{0:T(128)S(1)} %reshape.210), kind=kCustom, calls=%fused_computation | custom fusion | bytes 2098176 | tf_op jit(solution)/shard_map/gather | solution.py:94
  74.3 4.6 %convolution_bitcast_fusion = f32[8,384,1,256]{1,3,0,2:T(8,128)} fusion(f32[8,16,8,256]{3,2,1,0:T(8,128)S(1)} %bitcast.104, pred[8,16]{1,0:T(8,128)(4,1)S(1)} %compare_bitcast_fusion, f32[384,16,8]{0,2,1:T(8,128)S(1)} %bitcast.106), kind=kOutput, calls=%fused_computation.27 | convolution fusion | flops 1208221696 | bytes 4391040 | tf_op jit(solution)/shard_map/ykb,rkjbw->ryjw/dot_general | solution.py:98
  82.7 2.1 pad_maximum_fusion.4
  85.6 2.0 pad_maximum_fusion.5
  88.3 26.3 %reduce-scatter.2.cloned.1.call-done = f32[1,384,1,256]{1,3,0,2:T(8,128)} async-done(((f32[8,384,1,256]{1,3,0,2:T(8,128)}), f32[1,384,1,256]{1,3,0,2:T(8,128)}) %reduce-scatter.2.cloned.1.call-update) | async-done | bytes 393232 | tf_op jit(solution)/shard_map/reduce_scatter | solution.py:97
  114.6 1.9 copy.41
  116.5 6.9 %all-to-all-start = ((f32[1,384,1,256]{3,0,2,1:T(1,128)}), f32[1,384,1,256]{3,0,2,1:T(1,128)S(1)}, u32[]{:S(2)}, u32[]{:S(2)}) async-start(f32[1,384,1,256]{3,0,2,1:T(1,128)} %copy.41), calls=%async_computation.1 | async-start | bytes 786432 | tf_op jit(solution)/shard_map/all_to_all | solution.py:109
  123.9 2.4 copy.46
  126.3 3.4 %copy.47 = f32[24,192,128]{2,1,0:T(8,128)} copy(f32[24,192,128]{1,2,0:T(8,128)} %pad_maximum_fusion.5) | data formatting | bytes 4718592 | tf_op jit(solution)/shard_map/concatenate | solution.py:150
  130.4 1.4 pad_dynamic-update-slice_fusion.1
  133.4 2.5 reshape_squeeze.3
  135.9 5.7 %fusion.9 = f32[24,32,1536,1]{2,1,0,3:T(8,128)S(1)} fusion(f32[24,16,8,32]{3,2,0,1:T(8,128)} %reshape_squeeze.3, f32[128,1536]{1,0:T(8,128)S(1)} %copy-done), kind=kOutput, calls=%fused_computation.29 | convolution fusion | flops 1811939328 | bytes 5898240 | tf_op jit(solution)/shard_map/ykwc,kwx->ycx/dot_general | solution.py:114
  141.6 31.9 %fusion.7 = bf16[24,1536,64]{2,1,0:T(8,128)(2,1)} fusion(f32[24,32,1536,1]{2,1,0,3:T(8,128)S(1)} %fusion.9, f32[32,64]{1,0:T(8,128)S(1)} %copy-done.14), kind=kOutput, calls=%fused_computation.23 | convolution fusion | flops 905969664 | bytes 9445376 | tf_op jit(solution)/shard_map/ycx,cd->yxd/dot_general | solution.py:115
  173.5 12.7 %reshape.206 = bf16[24,768,128]{2,1,0:T(8,128)(2,1)} reshape(bf16[24,1536,64]{2,1,0:T(8,128)(2,1)} %fusion.7) | data formatting | bytes 9437184 | tf_op jit(solution)/shard_map/reshape | solution.py:116
  186.2 4.9 %fusion.3 = bf16[24,768,128]{2,1,0:T(8,128)(2,1)S(1)} fusion(bf16[24,768,128]{2,1,0:T(8,128)(2,1)} %reshape.206, pred[768,128]{1,0:T(8,128)(4,1)S(1)} %copy-done.11, pred[24]{0:T(512)(128)(4,1)S(1)} %copy-done.21), kind=kLoop, calls=%fused_computation.13 | loop fusion | flops 18874368 | bytes 9535512 | tf_op jit(solution)/shard_map/convert_element_type | solution.py:133
  191.2 3.8 %collective-permute-start = (bf16[1,768,128]{2,1,0:T(8,128)(2,1)S(1)}, bf16[1,768,128]{2,1,0:T(8,128)(2,1)S(1)}, u32[]{:S(2)}, u32[]{:S(2)}) collective-permute-start(bf16[1,768,128]{2,1,0:T(8,128)(2,1)S(1)} %get-tuple-element.11), channel_id=1, source_target_pairs={{0,1},{1,2},{2,3},{3,4},{4,5},{5,6},{6,7},{7,8},{8,9},{9,10},{10,1... | collective-permute-start | bytes 589832 | tf_op jit(solution)/shard_map/ppermute | solution.py:15
  198.2 4.4 %collective-permute-done.1 = bf16[1,768,128]{2,1,0:T(8,128)(2,1)S(1)} collective-permute-done((bf16[1,768,128]{2,1,0:T(8,128)(2,1)S(1)}, bf16[1,768,128]{2,1,0:T(8,128)(2,1)S(1)}, u32[]{:S(2)}, u32[]{:S(2)}) %collective-permute-start.1) | collective-permute-done | bytes 196640 | tf_op jit(solution)/shard_map/ppermute | solution.py:17
  203.3 4.0 %pad_slice_fusion.3 = (bf16[26,768,128]{2,1,0:T(8,128)(2,1)S(1)}, bf16[26,768,128]{2,1,0:T(8,128)(2,1)S(1)}) fusion(bf16[26,768,128]{2,1,0:T(8,128)(2,1)S(1)} %pad_maximum_fusion.2), kind=kLoop, calls=%fused_computation.20 | loop fusion | bytes 15335424 | tf_op jit(solution)/shard_map/slice | solution.py:48
  207.4 8.5 %fusion.21 = f32[24,768,128]{2,1,0:T(8,128)} fusion(bf16[3,384,128]{2,1,0:T(8,128)(2,1)S(1)} %copy-done.19, bf16[26,768,128]{2,1,0:T(8,128)(2,1)S(1)} %get-tuple-element.8, bf16[1,768,128]{2,1,0:T(8,128)(2,1)S(1)} %collective-permute-done.1, bf16[24,768,128]{2,1,0:T(8,128)(2,1)S(1)} %fusion.3, bf16[1,768,128]{2,1,0:T(8,128)(2,1)S(1)} %collective-permute-done, ...), kind=kOutput, calls=%fused_computation.48 | convolution fusion | flops 1888616448 | bytes 24870912 | tf_op jit(solution)/shard_map/ypk,kn->ypn/dot_general | solution.py:53
  215.9 7.4 %fusion.22 = f32[24,768,128]{2,1,0:T(8,128)} fusion(bf16[3,384,128]{2,1,0:T(8,128)(2,1)S(1)} %copy-done.19, bf16[26,768,128]{2,1,0:T(8,128)(2,1)S(1)} %get-tuple-element.8, bf16[1,768,128]{2,1,0:T(8,128)(2,1)S(1)} %collective-permute-done.1, bf16[24,768,128]{2,1,0:T(8,128)(2,1)S(1)} %fusion.3, bf16[1,768,128]{2,1,0:T(8,128)(2,1)S(1)} %collective-permute-done, ...), kind=kOutput, calls=%fused_computation.50 | convolution fusion | flops 1888616448 | bytes 24870912 | tf_op jit(solution)/shard_map/ypk,kn->ypn/dot_general | solution.py:53
  223.3 5.3 %mul.53 = f32[24,192,4,128]{3,2,1,0:T(4,128)} broadcast(f32[24,192,128]{2,1,0:T(8,128)S(1)} %copy.46), dimensions={0,1,3} | broadcast | bytes 11796480 | tf_op jit(solution)/shard_map/mul | solution.py:152
  228.6 7.0 %add.156 = f32[24,192,4,128]{3,2,1,0:T(4,128)} broadcast(f32[24,192,128]{2,1,0:T(8,128)} %copy.47), dimensions={0,1,3} | broadcast | bytes 11796480 | tf_op jit(solution)/shard_map/add | solution.py:152
  235.6 18.3 %fusion.5 = bf16[24,768,128]{2,1,0:T(8,128)(2,1)S(1)} fusion(f32[24,768,128]{2,1,0:T(8,128)} %bitcast.102, f32[24,768,128]{2,1,0:T(8,128)} %bitcast.101, f32[24,768,128]{2,1,0:T(8,128)} %fusion.22, f32[24,768,128]{2,1,0:T(8,128)} %fusion.21, pred[768,128]{1,0:T(8,128)(4,1)S(1)} %copy-done.11, pred[24]{0:T(512)(128)(4,1)S(1)} %copy-done.21, ...), kind=kOutput, calls=%fused_computation.15 | convolution fusion | flops 1914568704 | bytes 57999872 | tf_op jit(solution)/shard_map/ypk,kn->ypn/dot_general | solution.py:53
  253.9 3.3 %collective-permute-start.2 = (bf16[1,768,128]{2,1,0:T(8,128)(2,1)S(1)}, bf16[1,768,128]{2,1,0:T(8,128)(2,1)S(1)}, u32[]{:S(2)}, u32[]{:S(2)}) collective-permute-start(bf16[1,768,128]{2,1,0:T(8,128)(2,1)S(1)} %get-tuple-element.9), channel_id=1, source_target_pairs={{0,1},{1,2},{2,3},{3,4},{4,5},{5,6},{6,7},{7,8},{8,9},{9,10},{10,1... | collective-permute-start | bytes 589832 | tf_op jit(solution)/shard_map/ppermute | solution.py:15
  258.7 1.7 collective-permute-done.2
  260.4 4.4 %collective-permute-done.3 = bf16[1,768,128]{2,1,0:T(8,128)(2,1)S(1)} collective-permute-done((bf16[1,768,128]{2,1,0:T(8,128)(2,1)S(1)}, bf16[1,768,128]{2,1,0:T(8,128)(2,1)S(1)}, u32[]{:S(2)}, u32[]{:S(2)}) %collective-permute-start.3) | collective-permute-done | bytes 196640 | tf_op jit(solution)/shard_map/ppermute | solution.py:17
  265.5 4.0 %pad_slice_fusion.1 = (bf16[26,768,128]{2,1,0:T(8,128)(2,1)S(1)}, bf16[26,768,128]{2,1,0:T(8,128)(2,1)S(1)}) fusion(bf16[26,768,128]{2,1,0:T(8,128)(2,1)S(1)} %pad_maximum_fusion.3), kind=kLoop, calls=%fused_computation.18 | loop fusion | bytes 15335424 | tf_op jit(solution)/shard_map/slice | solution.py:48
  269.6 8.0 %fusion.19 = f32[24,768,128]{2,1,0:T(8,128)} fusion(bf16[3,384,128]{2,1,0:T(8,128)(2,1)S(1)} %constant_dynamic-update-slice_fusion.2, bf16[26,768,128]{2,1,0:T(8,128)(2,1)S(1)} %get-tuple-element.6, bf16[1,768,128]{2,1,0:T(8,128)(2,1)S(1)} %collective-permute-done.3, bf16[24,768,128]{2,1,0:T(8,128)(2,1)S(1)} %fusion.5, ...), kind=kOutput, calls=%fused_computation.43 | convolution fusion | flops 1888616448 | bytes 24870912 | tf_op jit(solution)/shard_map/ypk,kn->ypn/dot_general | solution.py:53
  277.6 7.4 %fusion.20 = f32[24,768,128]{2,1,0:T(8,128)} fusion(bf16[3,384,128]{2,1,0:T(8,128)(2,1)S(1)} %constant_dynamic-update-slice_fusion.2, bf16[26,768,128]{2,1,0:T(8,128)(2,1)S(1)} %get-tuple-element.6, bf16[1,768,128]{2,1,0:T(8,128)(2,1)S(1)} %collective-permute-done.3, bf16[24,768,128]{2,1,0:T(8,128)(2,1)S(1)} %fusion.5, ...), kind=kOutput, calls=%fused_computation.45 | convolution fusion | flops 1888616448 | bytes 24870912 | tf_op jit(solution)/shard_map/ypk,kn->ypn/dot_general | solution.py:53
  285.0 13.8 %fusion.6 = bf16[24,768,128]{2,1,0:T(8,128)(2,1)} fusion(f32[24,768,128]{2,1,0:T(8,128)} %fusion.20, f32[24,768,128]{2,1,0:T(8,128)} %fusion.19, pred[768,128]{1,0:T(8,128)(4,1)S(1)} %copy-done.11, pred[24]{0:T(512)(128)(4,1)S(1)} %copy-done.21, bf16[3,384,128]{2,1,0:T(8,128)(2,1)S(1)} %constant_dynamic-update-slice_fusion.2, ...), kind=kOutput, calls=%fused_computation.16 | convolution fusion | flops 1907490816 | bytes 43844096 | tf_op jit(solution)/shard_map/ypk,kn->ypn/dot_general | solution.py:53
  298.8 6.4 %reshape.207 = bf16[1,24,98304]{2,1,0:T(8,128)(2,1)} reshape(bf16[24,768,128]{2,1,0:T(8,128)(2,1)} %fusion.6) | data formatting | bytes 9437184 | tf_op jit(solution)/shard_map/reshape | solution.py:159
  (96 shorter events, 16.0 us)
Async XLA Ops:
  6.5 129.4 %copy-start = (f32[128,1536]{1,0:T(8,128)S(1)}, f32[128,1536]{1,0:T(8,128)}, u32[]{:S(2)}) copy-start(f32[128,1536]{1,0:T(8,128)} %param.16) | copy-start | bytes 2359300
  6.5 72.4 %copy-start.20 = (s32[8,2]{0,1:T(2,128)S(1)}, s32[8,2]{0,1:T(2,128)}, u32[]{:S(2)}) copy-start(s32[8,2]{0,1:T(2,128)} %param.13) | copy-start | bytes 196
  6.5 73.7 %copy-start.7 = (s32[1,48,192]{2,1,0:T(8,128)S(1)}, s32[1,48,192]{2,1,0:T(8,128)}, u32[]{:S(2)}) copy-start(s32[1,48,192]{2,1,0:T(8,128)} %param.14) | copy-start | bytes 110596
  6.5 75.0 %copy-start.12 = (bf16[3,3,64,64]{3,2,1,0:T(8,128)(2,1)S(1)}, bf16[3,3,64,64]{3,2,1,0:T(8,128)(2,1)}, u32[]{:S(2)}) copy-start(bf16[3,3,64,64]{3,2,1,0:T(8,128)(2,1)} %param.18) | copy-start | bytes 221188
  6.5 75.3 %copy-start.15 = (f32[16,64]{1,0:T(8,128)S(1)}, f32[16,64]{1,0:T(8,128)}, u32[]{:S(2)}) copy-start(f32[16,64]{1,0:T(8,128)} %param.20) | copy-start | bytes 12292
  6.5 64.2 %all-gather.2.cloned.1.call-start = ((), (), s32[]{:S(2)}) async-start(), calls=%async_computation.2 | async-start | bytes 6127616 | tf_op jit(solution)/shard_map/all_gather | solution.py:76
  7.3 107.3 %reduce-scatter.2.cloned.1.call-start = ((), (), s32[]{:S(2)}) async-start(), calls=%async_computation.3 | async-start | bytes 3538944 | tf_op jit(solution)/shard_map/reduce_scatter | solution.py:97
  74.3 10.5 %copy-start.16 = (f32[16,64]{1,0:T(8,128)S(1)}, f32[16,64]{1,0:T(8,128)}, u32[]{:S(2)}) copy-start(f32[16,64]{1,0:T(8,128)} %param.21) | copy-start | bytes 12292
  78.9 8.8 %copy-start.13 = (bf16[3,3,64,64]{3,2,1,0:T(8,128)(2,1)S(1)}, bf16[3,3,64,64]{3,2,1,0:T(8,128)(2,1)}, u32[]{:S(2)}) copy-start(bf16[3,3,64,64]{3,2,1,0:T(8,128)(2,1)} %param.19) | copy-start | bytes 221188
  81.9 41.5 %copy-start.18 = (bf16[3,384,128]{2,1,0:T(8,128)(2,1)}, bf16[3,384,128]{2,1,0:T(8,128)(2,1)S(1)}, u32[]{:S(2)}) copy-start(bf16[3,384,128]{2,1,0:T(8,128)(2,1)S(1)} %constant_dynamic-update-slice_fusion) | copy-start | bytes 884740
  116.5 16.2 %all-to-all-start = ((f32[1,384,1,256]{3,0,2,1:T(1,128)}), f32[1,384,1,256]{3,0,2,1:T(1,128)S(1)}, u32[]{:S(2)}, u32[]{:S(2)}) async-start(f32[1,384,1,256]{3,0,2,1:T(1,128)} %copy.41), calls=%async_computation.1 | async-start | bytes 786432 | tf_op jit(solution)/shard_map/all_to_all | solution.py:109
  132.6 9.0 %copy-start.14 = (f32[32,64]{1,0:T(8,128)S(1)}, f32[32,64]{1,0:T(8,128)}, u32[]{:S(2)}) copy-start(f32[32,64]{1,0:T(8,128)} %param.17) | copy-start | bytes 24580
  173.5 12.7 %copy-start.11 = (pred[768,128]{1,0:T(8,128)(4,1)S(1)}, pred[768,128]{1,0:T(8,128)(4,1)}, u32[]{:S(2)}) copy-start(pred[768,128]{1,0:T(8,128)(4,1)} %add_compare_fusion) | copy-start | bytes 294916
  173.5 12.7 %copy-start.21 = (pred[24]{0:T(512)(128)(4,1)S(1)}, pred[24]{0:T(512)(128)(4,1)}, u32[]{:S(2)}) copy-start(pred[24]{0:T(512)(128)(4,1)} %compare_and_fusion) | copy-start | bytes 76
  173.5 22.8 %copy-start.9 = (bf16[3,64,64]{2,1,0:T(8,128)(2,1)S(1)}, bf16[3,64,64]{2,1,0:T(8,128)(2,1)}, u32[]{:S(2)}) copy-start(bf16[3,64,64]{2,1,0:T(8,128)(2,1)} %get-tuple-element.21) | copy-start | bytes 73732
  173.5 22.8 %copy-start.10 = (bf16[3,64,64]{2,1,0:T(8,128)(2,1)S(1)}, bf16[3,64,64]{2,1,0:T(8,128)(2,1)}, u32[]{:S(2)}) copy-start(bf16[3,64,64]{2,1,0:T(8,128)(2,1)} %get-tuple-element.20) | copy-start | bytes 73732
  173.5 23.6 %copy-start.8 = (bf16[3,64,64]{2,1,0:T(8,128)(2,1)S(1)}, bf16[3,64,64]{2,1,0:T(8,128)(2,1)}, u32[]{:S(2)}) copy-start(bf16[3,64,64]{2,1,0:T(8,128)(2,1)} %get-tuple-element.19) | copy-start | bytes 73732
  191.1 24.8 %copy-start.2 = (bf16[24,768,128]{2,1,0:T(8,128)(2,1)}, bf16[24,768,128]{2,1,0:T(8,128)(2,1)S(1)}, u32[]{:S(2)}) copy-start(bf16[24,768,128]{2,1,0:T(8,128)(2,1)S(1)} %fusion.3) | copy-start | bytes 14155780
  191.2 7.0 %collective-permute-start = (bf16[1,768,128]{2,1,0:T(8,128)(2,1)S(1)}, bf16[1,768,128]{2,1,0:T(8,128)(2,1)S(1)}, u32[]{:S(2)}, u32[]{:S(2)}) collective-permute-start(bf16[1,768,128]{2,1,0:T(8,128)(2,1)S(1)} %get-tuple-element.11), channel_id=1, source_target_pairs={{0,1},{1,2},{2,3},{3,4},{4,5},{5,6},{6,7},{7,8},{8,9},{9,10},{10,1... | collective-permute-start | bytes 589832 | tf_op jit(solution)/shard_map/ppermute | solution.py:15
  195.0 7.6 %collective-permute-start.1 = (bf16[1,768,128]{2,1,0:T(8,128)(2,1)S(1)}, bf16[1,768,128]{2,1,0:T(8,128)(2,1)S(1)}, u32[]{:S(2)}, u32[]{:S(2)}) collective-permute-start(bf16[1,768,128]{2,1,0:T(8,128)(2,1)S(1)} %get-tuple-element.12), channel_id=1, source_target_pairs={{1,0},{2,1},{3,2},{4,3},{5,4},{6,5},{7,6},{8,7},{9,8},{10,9},{11,1... | collective-permute-start | bytes 589832 | tf_op jit(solution)/shard_map/ppermute | solution.py:17
  203.3 4.1 %copy-start.19 = (bf16[3,384,128]{2,1,0:T(8,128)(2,1)S(1)}, bf16[3,384,128]{2,1,0:T(8,128)(2,1)}, u32[]{:S(2)}) copy-start(bf16[3,384,128]{2,1,0:T(8,128)(2,1)} %copy-done.18) | copy-start | bytes 884740
  207.3 8.6 %copy-start.3 = (bf16[26,768,128]{2,1,0:T(8,128)(2,1)}, bf16[26,768,128]{2,1,0:T(8,128)(2,1)S(1)}, u32[]{:S(2)}) copy-start(bf16[26,768,128]{2,1,0:T(8,128)(2,1)S(1)} %get-tuple-element.7) | copy-start | bytes 15335428
  207.3 8.6 %copy-start.4 = (bf16[26,768,128]{2,1,0:T(8,128)(2,1)}, bf16[26,768,128]{2,1,0:T(8,128)(2,1)S(1)}, u32[]{:S(2)}) copy-start(bf16[26,768,128]{2,1,0:T(8,128)(2,1)S(1)} %get-tuple-element.8) | copy-start | bytes 15335428
  235.6 23.0 %copy-start.17 = (bf16[3,384,128]{2,1,0:T(8,128)(2,1)S(1)}, bf16[3,384,128]{2,1,0:T(8,128)(2,1)}, u32[]{:S(2)}) copy-start(bf16[3,384,128]{2,1,0:T(8,128)(2,1)} %maximum_dynamic-update-slice_fusion.2) | copy-start | bytes 884740
  253.9 6.5 %collective-permute-start.2 = (bf16[1,768,128]{2,1,0:T(8,128)(2,1)S(1)}, bf16[1,768,128]{2,1,0:T(8,128)(2,1)S(1)}, u32[]{:S(2)}, u32[]{:S(2)}) collective-permute-start(bf16[1,768,128]{2,1,0:T(8,128)(2,1)S(1)} %get-tuple-element.9), channel_id=1, source_target_pairs={{0,1},{1,2},{2,3},{3,4},{4,5},{5,6},{6,7},{7,8},{8,9},{9,10},{10,1... | collective-permute-start | bytes 589832 | tf_op jit(solution)/shard_map/ppermute | solution.py:15
  257.3 7.6 %collective-permute-start.3 = (bf16[1,768,128]{2,1,0:T(8,128)(2,1)S(1)}, bf16[1,768,128]{2,1,0:T(8,128)(2,1)S(1)}, u32[]{:S(2)}, u32[]{:S(2)}) collective-permute-start(bf16[1,768,128]{2,1,0:T(8,128)(2,1)S(1)} %get-tuple-element.10), channel_id=1, source_target_pairs={{1,0},{2,1},{3,2},{4,3},{5,4},{6,5},{7,6},{8,7},{9,8},{10,9},{11,1... | collective-permute-start | bytes 589832 | tf_op jit(solution)/shard_map/ppermute | solution.py:17
  269.6 8.1 %copy-start.5 = (bf16[26,768,128]{2,1,0:T(8,128)(2,1)}, bf16[26,768,128]{2,1,0:T(8,128)(2,1)S(1)}, u32[]{:S(2)}) copy-start(bf16[26,768,128]{2,1,0:T(8,128)(2,1)S(1)} %get-tuple-element.5) | copy-start | bytes 15335428
  269.6 8.1 %copy-start.6 = (bf16[26,768,128]{2,1,0:T(8,128)(2,1)}, bf16[26,768,128]{2,1,0:T(8,128)(2,1)S(1)}, u32[]{:S(2)}) copy-start(bf16[26,768,128]{2,1,0:T(8,128)(2,1)S(1)} %get-tuple-element.6) | copy-start | bytes 15335428
  269.6 15.4 %slice-start = ((s8[4718592]{0:T(1024)(128)(4,1)}), s8[4194304]{0:T(1024)(128)(4,1)S(1)}, s32[]{:S(2)}) async-start(s8[4718592]{0:T(1024)(128)(4,1)} %bitcast.99), calls=%async_computation.4 | async-start | bytes 8388608
  277.6 7.4 %slice-start.1 = ((s8[4718592]{0:T(1024)(128)(4,1)}), s8[524288]{0:T(1024)(128)(4,1)S(1)}, s32[]{:S(2)}) async-start(s8[4718592]{0:T(1024)(128)(4,1)} %bitcast.99), calls=%async_computation.5 | async-start | bytes 1048576
  285.0 20.3 %copy-start.1 = (f32[128,1536]{1,0:T(8,128)S(1)}, f32[128,1536]{1,0:T(8,128)}, u32[]{:S(2)}) copy-start(f32[128,1536]{1,0:T(8,128)} %param.16) | copy-start | bytes 2359300
Sparse Core Ops, SparseCore 0:
  9.5 61.2 all-gather.1
  79.0 35.5 reduce-scatter.1
where the time goes:
time: 314 us; the launch traced here: 312 us
  matrix products  107 us (34%)
  waiting for transfers between devices  98.8 us (31%)
  local copies, waits for them, and re-layouts  60.8 us (19%)
  starting transfers between devices  16.8 us (5%)
  between operations  15.2 us (5%)
  other arithmetic  13.4 us (4%)
    dot_general x6, matrix products, conv_pairs(): jnp.einsum('ypk,kn->ypn', stacked[shift_row:shift_row + out_rows], weight...  63.4 us
    all_gather x1, waiting for transfers between devices, local(): band = lax.all_gather(coarse, 'slab', axis=1, tiled=True)  60.9 us
    dot_general x1, matrix products, local(): jnp.einsum('ycx,cd->yxd', upsampled, lift, precision=lax.Precision.HIGHEST)  31.9 us
    reduce_scatter x1, waiting for transfers between devices, local(): lax.psum_scatter(jnp.einsum('ykb,rkjbw->ryjw', rows_full, blocks, precisi...  26.3 us
    reshape x1, local copies, waits for them, and re-layouts, local(): lifted = lifted.reshape(rows_dev, pair_count, 2 * channels)  12.7 us
    ppermute x2, waiting for transfers between devices, extended(): lax.ppermute(head, axis, [((i + 1) % count, i) for i in range(ends)])  8.81 us
    slice x2, local copies, waits for them, and re-layouts, conv_pairs(): widened[:, 0:pair_count]  8.07 us
    ppermute x2, starting transfers between devices, extended(): lax.ppermute(tail, axis, [(i, (i + 1) % count) for i in range(ends)])  7.18 us
  transfers between devices with their start and end apart: 7, of which 6 were waited for; matrix products, arithmetic and copies ran while one was open for 7% of the time, Pallas kernels for 0%

commit v1 on v0

v1 whole, which is shorter than its diff:
```python
import jax
import jax.numpy as jnp
from jax import lax
from jax.experimental import pallas as pl
from jax.experimental.pallas import tpu as pltpu
from jax.sharding import PartitionSpec as P

BF = jnp.bfloat16
F32 = jnp.float32
ROWS = 24
HALO = 32
PAIRS = 768


def split_hi_lo(value):
    hi = value.astype(BF)
    lo = (value - hi.astype(F32)).astype(BF)
    return hi, lo


def silu(value):
    half = 0.5 * value
    return half + half * jnp.tanh(half)


def build_conv_weights(kernel_ref, out_ref):
    empty = jnp.zeros((64, 64), F32)
    for row_in in range(4):
        for slot, pixel in enumerate((0, 1, 2, -1)):
            for row_out in range(2):
                parts = []
                for pixel_out in range(2):
                    p = row_in - row_out
                    q = pixel - pixel_out + 1
                    if 0 <= p <= 2 and 0 <= q <= 2:
                        parts.append(kernel_ref[p, q].astype(F32))
                    else:
                        parts.append(empty)
                out_ref[pl.ds(row_in * 256 + slot * 64, 64), pl.ds(row_out * 128, 128)] = jnp.concatenate(
                    parts, axis=1
                ).astype(BF)


def compute_kernel(
    sc_ref,
    rows_ref,
    lift_ref,
    uc_ref,
    k1_ref,
    k2_ref,
    onehot_ref,
    table_ref,
    out_ref,
    w1,
    w2,
    lifted,
    act_in,
    hid_in,
    fine,
    maps,
    shifted,
    result,
):
    start = sc_ref[0]
    valid_rows = sc_ref[1]
    valid_pairs = sc_ref[2]
    first_row = sc_ref[3]

    build_conv_weights(k1_ref, w1)
    build_conv_weights(k2_ref, w2)
    for tile_row in range(5):
        maps[tile_row] = jnp.dot(onehot_ref[tile_row], table_ref[...], preferred_element_type=F32)
    for place in range(16):
        slot = lax.rem(place + start, 16)
        block = rows_ref[slot]
        block = jnp.concatenate([block, block], axis=1)
        value = jnp.dot(block, lift_ref[...], preferred_element_type=F32)
        for w in range(4):
            lifted[pl.ds((w * 16 + place) * HALO, HALO), :] = value[:, w * 128 : (w + 1) * 128]

    zeros8 = jnp.zeros((8, 128), F32)
    for row in range(2):
        shifted[row, pl.ds(0, 8), :] = zeros8
        shifted[row, pl.ds(8 + PAIRS, 8), :] = zeros8
    pair_ids = lax.broadcasted_iota(jnp.int32, (PAIRS, 128), 0)
    lane_low = lax.broadcasted_iota(jnp.int32, (PAIRS, 128), 1) < 64
    col_valid = pair_ids < valid_pairs
    low16 = lax.broadcasted_iota(jnp.int32, (16, 128), 1) < 64

    def spread(row, value, dst_ref, pair):
        shifted[row, pl.ds(8, PAIRS), :] = value
        after = shifted[row, pl.ds(9, PAIRS), :]
        before = shifted[row, pl.ds(7, PAIRS), :]
        dst_ref[pair, :, pl.ds(row * 256, 128)] = value.astype(BF)
        dst_ref[pair, :, pl.ds(row * 256 + 128, 128)] = jnp.where(lane_low, after, before).astype(BF)

    def stage_one(pair, carry):
        sides = []
        for row in range(2):
            parts = []
            for w in range(4):
                got = lifted[pl.ds(w * 16 * HALO + pair * 2 + row, 16, stride=HALO), :]
                turned = pltpu.roll(got, 64, 1)
                parts += [
                    jnp.where(low16, got, 0.0),
                    jnp.where(low16, 0.0, got),
                    jnp.where(low16, turned, 0.0),
                    jnp.where(low16, 0.0, turned),
                ]
            side = jnp.concatenate(parts, axis=0).astype(BF)
            sides.append(jnp.concatenate([side, side], axis=0))
        value = jnp.dot(uc_ref[...], jnp.concatenate(sides, axis=1), preferred_element_type=F32)
        for row in range(2):
            global_row = first_row + pair * 2 + row
            keep = col_valid & ((global_row >= 0) & (global_row < valid_rows))
            rounded = jnp.where(keep, value[:, row * 128 : (row + 1) * 128], 0.0).astype(BF)
            fine[pair, :, pl.ds(row * 128, 128)] = rounded
            spread(row, silu(rounded.astype(F32)), act_in, pair)
        return carry

    lax.fori_loop(0, 14, stage_one, 0)

    def conv(src_ref, pair, w_ref):
        window = jnp.concatenate([src_ref[pair], src_ref[pair + 1]], axis=1)
        return jnp.dot(window, w_ref[...], preferred_element_type=F32)

    def stage_two(pair, carry):
        value = conv(act_in, pair, w1)
        for row in range(2):
            local_row = pair * 2 + row
            tile_row = lax.div(local_row + 7, 8)
            global_row = first_row + 1 + local_row
            gain = maps[tile_row, :, pl.ds(0, 128)]
            shift = maps[tile_row, :, pl.ds(128, 128)]
            keep = col_valid & ((global_row >= 0) & (global_row < valid_rows))
            moved = value[:, row * 128 : (row + 1) * 128] * gain + shift
            spread(row, jnp.where(keep, silu(moved), 0.0), hid_in, pair)
        return carry

    lax.fori_loop(0, 13, stage_two, 0)

    def stage_three(pair, carry):
        value = conv(hid_in, pair, w2)
        for row in range(2):
            global_row = first_row + 2 + pair * 2 + row
            keep = col_valid & (global_row < valid_rows)
            total = fine[pair + 1, :, pl.ds(row * 128, 128)].astype(F32) + value[:, row * 128 : (row + 1) * 128]
            at = pl.multiple_of((pair * 2 + row) * PAIRS, PAIRS)
            result[pl.ds(at, PAIRS), :] = jnp.where(keep, total, 0.0)
        return carry

    lax.fori_loop(0, 12, stage_three, 0)

    def emit(group, carry):
        for k in range(16):
            p = group * 16 + k
            got = [result[pl.ds(p + 8 * r * PAIRS, 8, stride=PAIRS), :] for r in range(3)]
            out_ref[:, pl.ds(pl.multiple_of(p * 128, 128), 128)] = jnp.concatenate(got, axis=0).astype(BF)
        return carry

    lax.fori_loop(0, PAIRS // 16, emit, 0)


def compute(scalars, rows, lift_w, uc, kernel_one, kernel_two, onehot, table):
    vmem = pl.BlockSpec(memory_space=pltpu.VMEM)
    return pl.pallas_call(
        compute_kernel,
        out_shape=jax.ShapeDtypeStruct((ROWS, PAIRS * 128), BF),
        in_specs=[pl.BlockSpec(memory_space=pltpu.SMEM)] + [vmem] * 7,
        out_specs=vmem,
        scratch_shapes=[
            pltpu.VMEM((1024, 256), BF),
            pltpu.VMEM((1024, 256), BF),
            pltpu.VMEM((4 * 16 * HALO, 128), F32),
            pltpu.VMEM((14, PAIRS, 512), BF),
            pltpu.VMEM((13, PAIRS, 512), BF),
            pltpu.VMEM((14, PAIRS, 256), BF),
            pltpu.VMEM((5, PAIRS, 256), F32),
            pltpu.VMEM((2, PAIRS + 16, 128), F32),
            pltpu.VMEM((ROWS * PAIRS, 128), F32),
        ],
        compiler_params=pltpu.CompilerParams(vmem_limit_bytes=63 * 1024 * 1024),
        name="block",
    )(scalars, rows, lift_w, uc, kernel_one, kernel_two, onehot, table)


def local(
    coarse,
    cover,
    sizes,
    tclass,
    up_rows,
    up_cols,
    lift,
    kernel_one,
    kernel_two,
    gain_table,
    shift_table,
):
    region = lax.axis_index("region")
    slab = lax.axis_index("slab")
    columns = jnp.transpose(coarse.astype(BF), (1, 0, 2, 3)).reshape(11, 32, 256)
    columns = jnp.concatenate([columns, jnp.zeros((5, 32, 256), BF)], axis=0)
    columns = jnp.concatenate([columns, columns], axis=0)
    columns = lax.dynamic_slice_in_dim(columns, lax.rem(5 * slab, 16), 16, 0)
    columns = lax.all_to_all(columns, "slab", split_axis=0, concat_axis=0, tiled=True)
    starts = cover[:, 0, 0, 2]
    place = jnp.remainder(slab - starts, 16)
    wanted = jnp.remainder(starts + place, 176) // 11
    picked = columns[wanted]
    mine = lax.all_to_all(picked, "region", split_axis=0, concat_axis=0, tiled=True)
    first_block = cover[region, 0, 0, 0] * 4 + cover[region, 0, 0, 1]
    patch = lax.dynamic_slice_in_dim(mine.reshape(256, 256), first_block * 8, 128, 0)
    padded_rows = jnp.pad(up_rows, ((2, 6), (0, 0)))
    rows_w = jnp.concatenate([padded_rows[24 * s : 24 * s + HALO] for s in range(16)], axis=0)
    rows_hi, rows_lo = split_hi_lo(rows_w)
    up = jnp.dot(
        jnp.concatenate([rows_hi, rows_lo], axis=1),
        jnp.concatenate([patch, patch], axis=0),
        preferred_element_type=F32,
    )
    up = up.astype(BF).reshape(16, HALO, 256)
    up = lax.all_to_all(up, "slab", split_axis=0, concat_axis=0, tiled=True)

    cols = up_cols.reshape(16, 4, 2, PAIRS, 2)
    variants = [cols[:, :, q, :, par] for q, par in ((0, 0), (1, 1), (1, 0), (0, 1))]
    uc = jnp.stack(variants, axis=0)
    uc = jnp.transpose(uc, (3, 2, 0, 1)).reshape(PAIRS, 256)
    uc = jnp.concatenate(split_hi_lo(uc), axis=1)
    lift_hi, lift_lo = split_hi_lo(lift)
    eye = jnp.eye(8, dtype=BF)
    lift_w = jnp.concatenate([jnp.kron(eye, lift_hi), jnp.kron(eye, lift_lo)], axis=0)

    tile_rows = 3 * slab - 1 + jnp.arange(5, dtype=jnp.int32)
    classes = tclass[0][jnp.clip(tile_rows, 0, 47)]
    onehot = (classes[..., None] == jnp.arange(32, dtype=jnp.int32) % 16).astype(BF)
    onehot = jnp.broadcast_to(onehot[:, :, None, :], (5, 192, 4, 32)).reshape(5, PAIRS, 32)
    table = jnp.concatenate([gain_table, gain_table, shift_table, shift_table], axis=1)
    table = jnp.concatenate(split_hi_lo(table), axis=0)
    scalars = jnp.stack(
        [
            lax.rem(cover[region, 0, 0, 2], 16),
            sizes[region, 0] * 24,
            sizes[region, 1] * 48,
            slab * 24 - 2,
        ]
    ).astype(jnp.int32)
    out = compute(scalars, up, lift_w, uc, kernel_one, kernel_two, onehot, table)
    return out[None]


def solution(mesh):
    return jax.shard_map(
        local,
        mesh=mesh,
        in_specs=(
            P("region", "slab", None, None),
            P(),
            P(),
            P("region", None, None),
            P(),
            P(),
            P(),
            P(),
            P(),
            P(),
            P(),
        ),
        out_specs=P("region", "slab", None),
        check_vma=False,
    )
```

time: 314 us -> 277 us (0.88)
  local copies, waits for them, and re-layouts: 60.8 us -> 196 us
  matrix products: 107 us -> 0.93 us
  waiting for transfers between devices: 98.8 us -> 7.79 us
  Pallas kernels: 0 us -> 39.7 us
  between operations: 15.2 us -> 4.62 us
  other arithmetic: 13.4 us -> 6.31 us
    slice x6, local copies, waits for them, and re-layouts: 9.73 us -> 124 us  [the longest x5 123 us: local(): cols[:, :, q, :, par]]
    dot_general x11 -> x1, matrix products: 107 us -> 0.93 us  [local(): jnp.dot(jnp.concatenate([rows_hi, rows_lo], axis=1), jnp.concatenate([pat...]
    all_gather x1 -> x0, waiting for transfers between devices: 60.9 us -> none  [local(): band = lax.all_gather(coarse, 'slab', axis=1, tiled=True)]
    pallas_call x0 -> x1, Pallas kernels: none -> 39.7 us  [compute(): pl.pallas_call(compute_kernel, out_shape=jax.ShapeDtypeStruct((ROWS, PAIR...]
    reshape x2, local copies, waits for them, and re-layouts: 19.1 us -> 53.5 us  [the longest x1 53.2 us: local(): cols = up_cols.reshape(16, 4, 2, PAIRS, 2)]
    reduce_scatter x1 -> x0, waiting for transfers between devices: 26.3 us -> none  [local(): lax.psum_scatter(jnp.einsum('ykb,rkjbw->ryjw', rows_full, blocks, precisi...]
    all_to_all x1 -> x3, starting transfers between devices: 6.94 us -> 19.7 us  [the longest x1 7.99 us: local(): lax.all_to_all(columns, 'slab', split_axis=0, concat_axis=0, tiled=True)]
    ppermute x4 -> x0, waiting for transfers between devices: 11 us -> none  [the longest x2 8.81 us: extended(): lax.ppermute(head, axis, [((i + 1) % count, i) for i in range(ends)])]
  transfers between devices with their start and end apart: 7 -> 3, of which waited for: 6 -> 1; matrix products, arithmetic and copies ran while one was open for 7% -> 72% of each run, Pallas kernels for 0% -> 0%
where the time goes in v1:
time: 277 us; the launch traced here: 275 us
  local copies, waits for them, and re-layouts  196 us (71%)
  Pallas kernels  39.7 us (14%)
  starting transfers between devices  19.7 us (7%)
  waiting for transfers between devices  7.79 us (3%)
  other arithmetic  6.31 us (2%)
  between operations  4.62 us (2%)
    slice x5, local copies, waits for them, and re-layouts, local(): cols[:, :, q, :, par]  123 us
    reshape x1, local copies, waits for them, and re-layouts, local(): cols = up_cols.reshape(16, 4, 2, PAIRS, 2)  53.2 us
    pallas_call x1, Pallas kernels, compute(): pl.pallas_call(compute_kernel, out_shape=jax.ShapeDtypeStruct((ROWS, PAIR...  39.7 us
    unnamed x24, local copies, waits for them, and re-layouts  12 us
    all_to_all x1, starting transfers between devices, local(): lax.all_to_all(columns, 'slab', split_axis=0, concat_axis=0, tiled=True)  7.99 us
    all_to_all x1, waiting for transfers between devices, local(): up = lax.all_to_all(up, 'slab', split_axis=0, concat_axis=0, tiled=True)  7.78 us
    all_to_all x1, starting transfers between devices, local(): up = lax.all_to_all(up, 'slab', split_axis=0, concat_axis=0, tiled=True)  7.21 us
  transfers between devices with their start and end apart: 3, of which 1 were waited for; matrix products, arithmetic and copies ran while one was open for 72% of the time, Pallas kernels for 0%

profile of v1, /device:TPU:0, one launch (start us, length us, event | category | flops | bytes accessed | tf_op | source)
XLA Modules:
  0.0 274.8 jit_solution(18286019129842201680)
XLA Ops:
  0.0 1.0 copy.61
  1.0 0.9 fusion.2
  2.0 8.0 %all-to-all-start = ((bf16[16,32,256]{2,1,0:T(8,128)(2,1)}), bf16[16,32,256]{2,1,0:T(8,128)(2,1)S(1)}, u32[]{:S(2)}, u32[]{:S(2)}) async-start(bf16[16,32,256]{2,1,0:T(8,128)(2,1)} %fusion.2), calls=%async_computation | async-start | bytes 524288 | tf_op jit(solution)/shard_map/all_to_all | solution.py:206
  10.0 0.9 fusion.10
  10.9 0.9 subtract_convert_fusion.2
  11.7 1.0 slice_reduce_fusion
  13.5 0.7 constant_dynamic-update-slice_fusion.14
  14.2 0.7 constant_dynamic-update-slice_fusion.13
  14.9 0.7 constant_dynamic-update-slice_fusion.12
  15.7 0.7 constant_dynamic-update-slice_fusion.11
  16.4 0.7 constant_dynamic-update-slice_fusion.10
  17.1 0.7 constant_dynamic-update-slice_fusion.9
  17.9 0.7 constant_dynamic-update-slice_fusion.8
  18.6 0.7 constant_dynamic-update-slice_fusion.7
  20.1 0.7 constant_dynamic-update-slice_fusion.5
  22.3 0.7 constant_dynamic-update-slice_fusion.2
  24.4 53.2 %reshape.185 = f32[16,4,2,768,2]{4,3,2,1,0:T(8,128)} reshape(f32[128,1536]{1,0:T(8,128)} %param.16) | data formatting | bytes 1572864 | tf_op jit(solution)/shard_map/reshape | solution.py:225
  77.7 64.2 %fusion.18 = (f32[16,4,1,768,1]{4,3,2,1,0:T(8,128)}, f32[16,4,1,768,1]{4,3,2,1,0:T(8,128)}, f32[16,4,1,768,1]{4,3,2,1,0:T(8,128)}, f32[16,4,1,768,1]{4,3,2,1,0:T(8,128)}) fusion(f32[16,4,2,768,2]{4,3,2,1,0:T(8,128)} %reshape.185), kind=kLoop, calls=%fused_computation.76 | loop fusion | bytes 1572864 | tf_op jit(solution)/shard_map/slice | solution.py:226
  141.9 14.7 %copy.51 = f32[16,4,1,768,1]{3,0,4,2,1:T(8,128)S(1)} copy(f32[16,4,1,768,1]{4,3,2,1,0:T(8,128)} %get-tuple-element.11) | data formatting | bytes 393216 | tf_op jit(solution)/shard_map/slice | solution.py:226
  156.6 14.7 %copy.52 = f32[16,4,1,768,1]{3,0,4,2,1:T(8,128)S(1)} copy(f32[16,4,1,768,1]{4,3,2,1,0:T(8,128)} %get-tuple-element.14) | data formatting | bytes 393216 | tf_op jit(solution)/shard_map/slice | solution.py:226
  171.3 14.7 %copy.53 = f32[16,4,1,768,1]{3,0,4,2,1:T(8,128)S(1)} copy(f32[16,4,1,768,1]{4,3,2,1,0:T(8,128)} %get-tuple-element.13) | data formatting | bytes 393216 | tf_op jit(solution)/shard_map/slice | solution.py:226
  186.0 14.7 %copy.54 = f32[16,4,1,768,1]{3,0,4,2,1:T(8,128)S(1)} copy(f32[16,4,1,768,1]{4,3,2,1,0:T(8,128)} %get-tuple-element.12) | data formatting | bytes 393216 | tf_op jit(solution)/shard_map/slice | solution.py:226
  202.0 1.0 pad_maximum_fusion.uc_ref
  203.1 0.8 pad_maximum_fusion.1.lift_ref
  203.9 1.2 gather_fusion
  205.1 4.5 %all-to-all-start.1 = ((bf16[8,32,256]{2,1,0:T(8,128)(2,1)}), bf16[8,32,256]{2,1,0:T(8,128)(2,1)S(1)}, u32[]{:S(2)}, u32[]{:S(2)}) async-start(bf16[8,32,256]{2,1,0:T(8,128)(2,1)} %gather_fusion), calls=%async_computation.1 | async-start | bytes 262144 | tf_op jit(solution)/shard_map/all_to_all | solution.py:211
  209.6 1.3 constant_dynamic-slice_fusion.1
  216.6 0.9 convolution_convert_fusion
  217.5 7.2 %all-to-all-start.2 = ((bf16[16,32,256]{2,1,0:T(8,128)(2,1)}), bf16[16,32,256]{2,1,0:T(8,128)(2,1)S(1)}, u32[]{:S(2)}, u32[]{:S(2)}) async-start(bf16[16,32,256]{2,1,0:T(8,128)(2,1)} %bitcast.10), calls=%async_computation.2 | async-start | bytes 524288 | tf_op jit(solution)/shard_map/all_to_all | solution.py:223
  226.2 7.8 %all-to-all-done.2.rows_ref = bf16[16,32,256]{2,1,0:T(8,128)(2,1)S(1)} async-done(((bf16[16,32,256]{2,1,0:T(8,128)(2,1)}), bf16[16,32,256]{2,1,0:T(8,128)(2,1)S(1)}, u32[]{:S(2)}, u32[]{:S(2)}) %all-to-all-start.2) | async-done | bytes 262176 | tf_op jit(solution)/shard_map/all_to_all | solution.py:223
  233.9 1.2 broadcast_in_dim.13
  235.1 39.7 %block.1 = bf16[24,98304]{1,0:T(8,128)(2,1)} custom-call(s32[4]{0:T(128)} %pad_add_fusion.sc_ref, bf16[16,32,256]{2,1,0:T(8,128)(2,1)} %copy-done.1, bf16[512,512]{1,0:T(8,128)(2,1)} %pad_maximum_fusion.1.lift_ref, bf16[768,512]{1,0:T(8,128)(2,1)} %pad_maximum_fusion.uc_ref, bf16[3,3,64,64]{3,2,1,0:T(8,128)(2,1)} %k1_ref.1, bf16[3,3,64,64]{3,2,1,0:T(8,128)(2,1)} %k2_ref.1, ...), custom_call_target="tpu_custom_call" | custom-call | tf_op jit(solution)/shard_map/block/pallas_call | solution.py:166
  (38 shorter events, 8.4 us)
Async XLA Ops:
  0.0 225.4 %copy-start = (s32[1,48,192]{2,1,0:T(8,128)S(1)}, s32[1,48,192]{2,1,0:T(8,128)}, u32[]{:S(2)}) copy-start(s32[1,48,192]{2,1,0:T(8,128)} %param.14) | copy-start | bytes 110596
  2.0 201.9 %all-to-all-start = ((bf16[16,32,256]{2,1,0:T(8,128)(2,1)}), bf16[16,32,256]{2,1,0:T(8,128)(2,1)S(1)}, u32[]{:S(2)}, u32[]{:S(2)}) async-start(bf16[16,32,256]{2,1,0:T(8,128)(2,1)} %fusion.2), calls=%async_computation | async-start | bytes 524288 | tf_op jit(solution)/shard_map/all_to_all | solution.py:206
  171.3 29.9 %copy-start.2 = (f32[32,64]{1,0:T(8,128)S(1)}, f32[32,64]{1,0:T(8,128)}, u32[]{:S(2)}) copy-start(f32[32,64]{1,0:T(8,128)} %param.17) | copy-start | bytes 24580
  186.0 28.1 %copy-start.3 = (s32[8,2]{0,1:T(2,128)S(1)}, s32[8,2]{0,1:T(2,128)}, u32[]{:S(2)}) copy-start(s32[8,2]{0,1:T(2,128)} %param.13) | copy-start | bytes 196
  205.1 11.5 %all-to-all-start.1 = ((bf16[8,32,256]{2,1,0:T(8,128)(2,1)}), bf16[8,32,256]{2,1,0:T(8,128)(2,1)S(1)}, u32[]{:S(2)}, u32[]{:S(2)}) async-start(bf16[8,32,256]{2,1,0:T(8,128)(2,1)} %gather_fusion), calls=%async_computation.1 | async-start | bytes 262144 | tf_op jit(solution)/shard_map/all_to_all | solution.py:211
  217.5 16.4 %all-to-all-start.2 = ((bf16[16,32,256]{2,1,0:T(8,128)(2,1)}), bf16[16,32,256]{2,1,0:T(8,128)(2,1)S(1)}, u32[]{:S(2)}, u32[]{:S(2)}) async-start(bf16[16,32,256]{2,1,0:T(8,128)(2,1)} %bitcast.10), calls=%async_computation.2 | async-start | bytes 524288 | tf_op jit(solution)/shard_map/all_to_all | solution.py:223
  233.9 1.2 copy-start.1

commit v2 on v1

--- a/solution.py
+++ b/solution.py
@@ -41,18 +41,67 @@
                 ).astype(BF)
 
 
+def prepare_columns(cols_ref, split, uc):
+    source = lax.broadcasted_iota(jnp.int32, (256, 256), 0)
+    target = lax.broadcasted_iota(jnp.int32, (256, 256), 1)
+    chosen = jnp.where(target < 128, 2 * target, 2 * target - 255)
+    select = (source == chosen).astype(F32).astype(BF)
+    for chunk in range(6):
+        halves = split_hi_lo(cols_ref[:, pl.ds(chunk * 256, 256)])
+        for part in range(2):
+            value = jnp.dot(halves[part], select, preferred_element_type=F32)
+            split[pl.ds(part * 256, 128), :] = value[:, :128]
+            split[pl.ds(part * 256 + 128, 128), :] = value[:, 128:]
+        for part in range(2):
+            pieces = []
+            for w in range(4):
+                for q, parity in ((0, 0), (1, 1), (1, 0), (0, 1)):
+                    pieces.append(split[pl.ds(part * 256 + parity * 128 + 2 * w + q, 16, stride=8), :])
+            block = jnp.concatenate(pieces, axis=0).T
+            uc[pl.ds(chunk * 128, 128), pl.ds(part * 256, 256)] = block.astype(BF)
+
+
+def prepare_lift(lift_ref, lift_w):
+    empty = jnp.zeros((32, 64), F32)
+    lift_w[...] = jnp.zeros_like(lift_w)
+    for part, value in enumerate(split_hi_lo(lift_ref[...])):
+        value = value.astype(F32)
+        sides = (jnp.concatenate([value, empty], axis=1), jnp.concatenate([empty, value], axis=1))
+        for bw in range(8):
+            lift_w[pl.ds(part * 256 + bw * 32, 32), pl.ds(bw // 2 * 128, 128)] = sides[bw % 2].astype(BF)
+
+
+def prepare_maps(class_ref, gain_ref, shift_ref, maps):
+    gain, shift = gain_ref[...], shift_ref[...]
+    table = jnp.concatenate(split_hi_lo(jnp.concatenate([gain, gain, shift, shift], axis=1)), axis=0)
+    owner = lax.broadcasted_iota(jnp.int32, (192, PAIRS), 1) // 4
+    widen = (owner == lax.broadcasted_iota(jnp.int32, (192, PAIRS), 0)).astype(F32).astype(BF)
+    ids = lax.broadcasted_iota(jnp.int32, (32, 192), 0) % 16
+    hots = []
+    for tile_row in range(5):
+        hots.append((class_ref[pl.ds(tile_row, 1), :] == ids).astype(F32))
+    wide = jnp.dot(jnp.concatenate(hots, axis=0).astype(BF), widen, preferred_element_type=F32)
+    for tile_row in range(5):
+        hot = wide[tile_row * 32 : (tile_row + 1) * 32].T.astype(BF)
+        maps[tile_row] = jnp.dot(hot, table, preferred_element_type=F32)
+
+
 def compute_kernel(
     sc_ref,
     rows_ref,
     lift_ref,
-    uc_ref,
+    cols_ref,
     k1_ref,
     k2_ref,
-    onehot_ref,
-    table_ref,
+    class_ref,
+    gain_ref,
+    shift_ref,
     out_ref,
     w1,
     w2,
+    lift_w,
+    split,
+    uc,
     lifted,
     act_in,
     hid_in,
@@ -68,13 +117,14 @@
 
     build_conv_weights(k1_ref, w1)
     build_conv_weights(k2_ref, w2)
-    for tile_row in range(5):
-        maps[tile_row] = jnp.dot(onehot_ref[tile_row], table_ref[...], preferred_element_type=F32)
+    prepare_columns(cols_ref, split, uc)
+    prepare_lift(lift_ref, lift_w)
+    prepare_maps(class_ref, gain_ref, shift_ref, maps)
     for place in range(16):
         slot = lax.rem(place + start, 16)
         block = rows_ref[slot]
         block = jnp.concatenate([block, block], axis=1)
-        value = jnp.dot(block, lift_ref[...], preferred_element_type=F32)
+        value = jnp.dot(block, lift_w[...], preferred_element_type=F32)
         for w in range(4):
             lifted[pl.ds((w * 16 + place) * HALO, HALO), :] = value[:, w * 128 : (w + 1) * 128]
 
@@ -109,7 +159,7 @@
                 ]
             side = jnp.concatenate(parts, axis=0).astype(BF)
             sides.append(jnp.concatenate([side, side], axis=0))
-        value = jnp.dot(uc_ref[...], jnp.concatenate(sides, axis=1), preferred_element_type=F32)
+        value = jnp.dot(uc[...], jnp.concatenate(sides, axis=1), preferred_element_type=F32)
         for row in range(2):
             global_row = first_row + pair * 2 + row
             keep = col_valid & ((global_row >= 0) & (global_row < valid_rows))
@@ -161,16 +211,19 @@
     lax.fori_loop(0, PAIRS // 16, emit, 0)
 
 
-def compute(scalars, rows, lift_w, uc, kernel_one, kernel_two, onehot, table):
+def compute(scalars, *operands):
     vmem = pl.BlockSpec(memory_space=pltpu.VMEM)
     return pl.pallas_call(
         compute_kernel,
         out_shape=jax.ShapeDtypeStruct((ROWS, PAIRS * 128), BF),
-        in_specs=[pl.BlockSpec(memory_space=pltpu.SMEM)] + [vmem] * 7,
+        in_specs=[pl.BlockSpec(memory_space=pltpu.SMEM)] + [vmem] * len(operands),
         out_specs=vmem,
         scratch_shapes=[
             pltpu.VMEM((1024, 256), BF),
             pltpu.VMEM((1024, 256), BF),
+            pltpu.VMEM((512, 512), BF),
+            pltpu.VMEM((512, 128), F32),
+            pltpu.VMEM((PAIRS, 512), BF),
             pltpu.VMEM((4 * 16 * HALO, 128), F32),
             pltpu.VMEM((14, PAIRS, 512), BF),
             pltpu.VMEM((13, PAIRS, 512), BF),
@@ -181,7 +234,7 @@
         ],
         compiler_params=pltpu.CompilerParams(vmem_limit_bytes=63 * 1024 * 1024),
         name="block",
-    )(scalars, rows, lift_w, uc, kernel_one, kernel_two, onehot, table)
+    )(scalars, *operands)
 
 
 def local(
@@ -213,30 +266,14 @@
     patch = lax.dynamic_slice_in_dim(mine.reshape(256, 256), first_block * 8, 128, 0)
     padded_rows = jnp.pad(up_rows, ((2, 6), (0, 0)))
     rows_w = jnp.concatenate([padded_rows[24 * s : 24 * s + HALO] for s in range(16)], axis=0)
-    rows_hi, rows_lo = split_hi_lo(rows_w)
-    up = jnp.dot(
-        jnp.concatenate([rows_hi, rows_lo], axis=1),
-        jnp.concatenate([patch, patch], axis=0),
-        preferred_element_type=F32,
-    )
+    rows_hi = lax.reduce_precision(rows_w, 8, 7)
+    rows_w = jnp.concatenate([rows_hi.astype(BF), (rows_w - rows_hi).astype(BF)], axis=1)
+    up = jnp.dot(rows_w, jnp.concatenate([patch, patch], axis=0), preferred_element_type=F32)
     up = up.astype(BF).reshape(16, HALO, 256)
     up = lax.all_to_all(up, "slab", split_axis=0, concat_axis=0, tiled=True)
 
-    cols = up_cols.reshape(16, 4, 2, PAIRS, 2)
-    variants = [cols[:, :, q, :, par] for q, par in ((0, 0), (1, 1), (1, 0), (0, 1))]
-    uc = jnp.stack(variants, axis=0)
-    uc = jnp.transpose(uc, (3, 2, 0, 1)).reshape(PAIRS, 256)
-    uc = jnp.concatenate(split_hi_lo(uc), axis=1)
-    lift_hi, lift_lo = split_hi_lo(lift)
-    eye = jnp.eye(8, dtype=BF)
-    lift_w = jnp.concatenate([jnp.kron(eye, lift_hi), jnp.kron(eye, lift_lo)], axis=0)
-
-    tile_rows = 3 * slab - 1 + jnp.arange(5, dtype=jnp.int32)
-    classes = tclass[0][jnp.clip(tile_rows, 0, 47)]
-    onehot = (classes[..., None] == jnp.arange(32, dtype=jnp.int32) % 16).astype(BF)
-    onehot = jnp.broadcast_to(onehot[:, :, None, :], (5, 192, 4, 32)).reshape(5, PAIRS, 32)
-    table = jnp.concatenate([gain_table, gain_table, shift_table, shift_table], axis=1)
-    table = jnp.concatenate(split_hi_lo(table), axis=0)
+    tile_rows = jnp.clip(3 * slab - 1 + jnp.arange(8, dtype=jnp.int32), 0, 47)
+    classes = tclass[0][tile_rows]
     scalars = jnp.stack(
         [
             lax.rem(cover[region, 0, 0, 2], 16),
@@ -245,7 +282,7 @@
             slab * 24 - 2,
         ]
     ).astype(jnp.int32)
-    out = compute(scalars, up, lift_w, uc, kernel_one, kernel_two, onehot, table)
+    out = compute(scalars, up, lift, up_cols, kernel_one, kernel_two, classes, gain_table, shift_table)
     return out[None]
 
 

time: 277 us -> 93 us (0.34)
  local copies, waits for them, and re-layouts: 196 us -> 18.7 us
  other arithmetic: 6.31 us -> 1.64 us
    slice x5 -> x0, local copies, waits for them, and re-layouts: 123 us -> none  [local(): cols[:, :, q, :, par]]
    reshape x2 -> x0, local copies, waits for them, and re-layouts: 53.5 us -> none  [the longest x1 53.2 us: local(): cols = up_cols.reshape(16, 4, 2, PAIRS, 2)]
    all_to_all x1, waiting for transfers between devices: 7.78 us -> 3.02 us  [local(): up = lax.all_to_all(up, 'slab', split_axis=0, concat_axis=0, tiled=True)]
    all_to_all x1, waiting for transfers between devices: 0.01 us -> 3.47 us  [local(): lax.all_to_all(picked, 'region', split_axis=0, concat_axis=0, tiled=True)]
    unnamed x24 -> x22, local copies, waits for them, and re-layouts: 12 us -> 12.7 us
  transfers between devices with their start and end apart: 3 -> 3, of which waited for: 1 -> 2; matrix products, arithmetic and copies ran while one was open for 72% -> 18% of each run, Pallas kernels for 0% -> 0%
where the time goes in v2:
time: 93 us; the launch traced here: 91.5 us
  Pallas kernels  39.6 us (43%)
  starting transfers between devices  19.7 us (21%)
  local copies, waits for them, and re-layouts  18.7 us (20%)
  waiting for transfers between devices  6.49 us (7%)
  between operations  4.45 us (5%)
  other arithmetic  1.64 us (2%)
  matrix products  0.94 us (1%)
    pallas_call x1, Pallas kernels, compute(): pl.pallas_call(compute_kernel, out_shape=jax.ShapeDtypeStruct((ROWS, PAIR...  39.6 us
    unnamed x22, local copies, waits for them, and re-layouts  12.7 us
    all_to_all x1, starting transfers between devices, local(): lax.all_to_all(columns, 'slab', split_axis=0, concat_axis=0, tiled=True)  7.99 us
    all_to_all x1, starting transfers between devices, local(): up = lax.all_to_all(up, 'slab', split_axis=0, concat_axis=0, tiled=True)  7.21 us
    all_to_all x1, starting transfers between devices, local(): lax.all_to_all(picked, 'region', split_axis=0, concat_axis=0, tiled=True)  4.47 us
    all_to_all x1, waiting for transfers between devices, local(): lax.all_to_all(picked, 'region', split_axis=0, concat_axis=0, tiled=True)  3.47 us
    all_to_all x1, waiting for transfers between devices, local(): up = lax.all_to_all(up, 'slab', split_axis=0, concat_axis=0, tiled=True)  3.02 us
  transfers between devices with their start and end apart: 3, of which 2 were waited for; matrix products, arithmetic and copies ran while one was open for 18% of the time, Pallas kernels for 0%

profile of v2, /device:TPU:0, one launch (start us, length us, event | category | flops | bytes accessed | tf_op | source)
XLA Modules:
  0.0 91.5 jit_solution(17382967061329173404)
XLA Ops:
  0.0 1.0 %copy.16 = bf16[4,11,8,256]{3,2,0,1:T(8,128)(2,1)S(1)} copy(f32[4,11,8,256]{3,2,1,0:T(8,128)} %param.11) | data formatting | bytes 540672 | tf_op args[0]
  1.1 0.9 %fusion.3 = bf16[16,32,256]{2,1,0:T(8,128)(2,1)} fusion(s32[]{:T(128)S(6)} %select_n.71, bf16[11,32,256]{2,1,0:T(8,128)(2,1)S(1)} %bitcast.33, bf16[5,32,256]{2,1,0:T(8,128)(2,1)S(1)} %broadcast_in_dim.8), kind=kLoop, calls=%fused_computation.13 | loop fusion | flops 393216 | bytes 524292 | tf_op jit(solution)/shard_map/concatenate | solution.py:257
  2.0 8.0 %all-to-all-start = ((bf16[16,32,256]{2,1,0:T(8,128)(2,1)}), bf16[16,32,256]{2,1,0:T(8,128)(2,1)S(1)}, u32[]{:S(2)}, u32[]{:S(2)}) async-start(bf16[16,32,256]{2,1,0:T(8,128)(2,1)} %fusion.3), calls=%async_computation | async-start | bytes 524288 | tf_op jit(solution)/shard_map/all_to_all | solution.py:259
  10.0 1.0 %slice_reduce_fusion = s32[8]{0:T(128)S(1)} fusion(s32[8,16,16,3]{2,1,3,0:T(8,128)} %param.12), kind=kLoop, calls=%fused_computation.41 | loop fusion | bytes 64 | tf_op jit(solution)/shard_map/slice | solution.py:260
  11.0 0.7 constant_dynamic-update-slice_fusion.15
  11.7 0.7 constant_dynamic-update-slice_fusion.14
  12.5 0.7 constant_dynamic-update-slice_fusion.13
  13.2 0.7 constant_dynamic-update-slice_fusion.12
  13.9 0.7 constant_dynamic-update-slice_fusion.11
  14.7 0.7 constant_dynamic-update-slice_fusion.10
  15.4 0.7 constant_dynamic-update-slice_fusion.9
  16.1 0.7 constant_dynamic-update-slice_fusion.8
  16.8 0.7 constant_dynamic-update-slice_fusion.7
  17.6 0.7 constant_dynamic-update-slice_fusion.6
  18.3 0.7 constant_dynamic-update-slice_fusion.5
  19.0 0.7 constant_dynamic-update-slice_fusion.4
  19.8 0.7 constant_dynamic-update-slice_fusion.3
  20.5 0.7 constant_dynamic-update-slice_fusion.2
  21.2 0.7 constant_dynamic-update-slice_fusion.1
  22.0 0.7 constant_dynamic-update-slice_fusion
  22.7 1.2 %gather_fusion = bf16[8,32,256]{2,1,0:T(8,128)(2,1)} fusion(bf16[16,32,256]{2,1,0:T(8,128)(2,1)S(1)} %all-to-all-done, s32[1024]{0:T(1024)S(1)} %pad_clamp_fusion.1), kind=kCustom, calls=%fused_computation | custom fusion | bytes 262176 | tf_op jit(solution)/shard_map/gather | solution.py:263
  23.9 4.5 %all-to-all-start.1 = ((bf16[8,32,256]{2,1,0:T(8,128)(2,1)}), bf16[8,32,256]{2,1,0:T(8,128)(2,1)S(1)}, u32[]{:S(2)}, u32[]{:S(2)}) async-start(bf16[8,32,256]{2,1,0:T(8,128)(2,1)} %gather_fusion), calls=%async_computation.1 | async-start | bytes 262144 | tf_op jit(solution)/shard_map/all_to_all | solution.py:264
  28.5 1.3 %constant_dynamic-slice_fusion.1 = (s32[1,1,1,1]{2,1,3,0:T(1,128)}, s32[1,1,1,1]{2,1,3,0:T(1,128)}, s32[1,1,1,1]{2,1,3,0:T(1,128)}) fusion(s32[8,16,16,3]{2,1,3,0:T(8,128)} %param.12, s32[]{:T(128)S(6)} %select_n.70), kind=kLoop, calls=%fused_computation.45 | loop fusion | bytes 28 | tf_op jit(solution)/shard_map/dynamic_slice | solution.py:265
  31.0 3.5 %all-to-all-done.1 = bf16[8,32,256]{2,1,0:T(8,128)(2,1)S(1)} async-done(((bf16[8,32,256]{2,1,0:T(8,128)(2,1)}), bf16[8,32,256]{2,1,0:T(8,128)(2,1)S(1)}, u32[]{:S(2)}, u32[]{:S(2)}) %all-to-all-start.1) | async-done | bytes 131104 | tf_op jit(solution)/shard_map/all_to_all | solution.py:264
  34.5 0.9 %convolution_convert_fusion = bf16[512,256]{1,0:T(8,128)(2,1)} fusion(bf16[512,128]{1,0:T(8,128)(2,1)S(1)} %get-tuple-element.6, bf16[512,128]{1,0:T(8,128)(2,1)S(1)} %get-tuple-element.5, bf16[128,256]{1,0:T(8,128)(2,1)S(1)} %constant_dynamic-slice_fusion), kind=kOutput, calls=%fused_computation.2 | convolution fusion | flops 68026368 | bytes 589824 | tf_op jit(solution)/shard_map/dot_general | solution.py:271
  35.5 7.2 %all-to-all-start.2 = ((bf16[16,32,256]{2,1,0:T(8,128)(2,1)}), bf16[16,32,256]{2,1,0:T(8,128)(2,1)S(1)}, u32[]{:S(2)}, u32[]{:S(2)}) async-start(bf16[16,32,256]{2,1,0:T(8,128)(2,1)} %bitcast.10), calls=%async_computation.2 | async-start | bytes 524288 | tf_op jit(solution)/shard_map/all_to_all | solution.py:273
  44.6 0.6 constant_dynamic-slice_fusion.3
  46.4 1.2 %gather_fusion.1 = s32[8,192]{1,0:T(8,128)} fusion(s32[48,192]{1,0:T(8,128)S(1)} %bitcast.32, s32[1024]{0:T(1024)S(1)} %pad_clamp_fusion), kind=kCustom, calls=%fused_computation.1 | custom fusion | bytes 12320 | tf_op jit(solution)/shard_map/gather | solution.py:276
  47.6 0.6 pad_add_fusion.sc_ref
  48.2 3.0 %all-to-all-done.2.rows_ref = bf16[16,32,256]{2,1,0:T(8,128)(2,1)S(1)} async-done(((bf16[16,32,256]{2,1,0:T(8,128)(2,1)}), bf16[16,32,256]{2,1,0:T(8,128)(2,1)S(1)}, u32[]{:S(2)}, u32[]{:S(2)}) %all-to-all-start.2) | async-done | bytes 262176 | tf_op jit(solution)/shard_map/all_to_all | solution.py:273
  51.2 0.7 copy-done.1
  51.9 39.6 %block.1 = bf16[24,98304]{1,0:T(8,128)(2,1)} custom-call(s32[4]{0:T(128)} %pad_add_fusion.sc_ref, bf16[16,32,256]{2,1,0:T(8,128)(2,1)} %copy-done.1, f32[32,64]{1,0:T(8,128)} %lift_ref.1, f32[128,1536]{1,0:T(8,128)} %cols_ref.1, bf16[3,3,64,64]{3,2,1,0:T(8,128)(2,1)} %k1_ref.1, bf16[3,3,64,64]{3,2,1,0:T(8,128)(2,1)} %k2_ref.1, s32[8,192]{1,0:T(8,128)} %gather_fusion.1, ...), custom_call_target="tpu_custom_call" | custom-call | tf_op jit(solution)/shard_map/block/pallas_call | solution.py:216
  (13 shorter events, 0.1 us)
Async XLA Ops:
  0.0 46.4 %copy-start = (s32[1,48,192]{2,1,0:T(8,128)S(1)}, s32[1,48,192]{2,1,0:T(8,128)}, u32[]{:S(2)}) copy-start(s32[1,48,192]{2,1,0:T(8,128)} %param.14) | copy-start | bytes 110596
  0.0 44.6 %copy-start.2 = (s32[8,2]{0,1:T(2,128)S(1)}, s32[8,2]{0,1:T(2,128)}, u32[]{:S(2)}) copy-start(s32[8,2]{0,1:T(2,128)} %param.13) | copy-start | bytes 196
  2.0 20.7 %all-to-all-start = ((bf16[16,32,256]{2,1,0:T(8,128)(2,1)}), bf16[16,32,256]{2,1,0:T(8,128)(2,1)S(1)}, u32[]{:S(2)}, u32[]{:S(2)}) async-start(bf16[16,32,256]{2,1,0:T(8,128)(2,1)} %fusion.3), calls=%async_computation | async-start | bytes 524288 | tf_op jit(solution)/shard_map/all_to_all | solution.py:259
  23.9 10.6 %all-to-all-start.1 = ((bf16[8,32,256]{2,1,0:T(8,128)(2,1)}), bf16[8,32,256]{2,1,0:T(8,128)(2,1)S(1)}, u32[]{:S(2)}, u32[]{:S(2)}) async-start(bf16[8,32,256]{2,1,0:T(8,128)(2,1)} %gather_fusion), calls=%async_computation.1 | async-start | bytes 262144 | tf_op jit(solution)/shard_map/all_to_all | solution.py:264
  35.5 15.7 %all-to-all-start.2 = ((bf16[16,32,256]{2,1,0:T(8,128)(2,1)}), bf16[16,32,256]{2,1,0:T(8,128)(2,1)S(1)}, u32[]{:S(2)}, u32[]{:S(2)}) async-start(bf16[16,32,256]{2,1,0:T(8,128)(2,1)} %bitcast.10), calls=%async_computation.2 | async-start | bytes 524288 | tf_op jit(solution)/shard_map/all_to_all | solution.py:273
  51.2 0.7 copy-start.1

commit v3 on v2

--- a/solution.py
+++ b/solution.py
@@ -39,6 +39,207 @@
                 out_ref[pl.ds(row_in * 256 + slot * 64, 64), pl.ds(row_out * 128, 128)] = jnp.concatenate(
                     parts, axis=1
                 ).astype(BF)
+
+
+MESH = pl.DeviceIdType.MESH
+
+
+def exchange_kernel(
+    heads_ref,
+    coarse_ref,
+    up_ref,
+    out_ref,
+    cols_send,
+    cols_recv,
+    pick_send,
+    pick_recv,
+    rows_send,
+    rows_recv,
+    padded,
+    weights,
+    send_one,
+    recv_one,
+    send_two,
+    recv_two,
+    send_three,
+    recv_three,
+):
+    region = lax.axis_index("region")
+    slab = lax.axis_index("slab")
+
+    barrier = pltpu.get_barrier_semaphore()
+
+    def greet_slab(step, carry):
+        pl.semaphore_signal(barrier, inc=1, device_id={"slab": lax.rem(slab + step, 16)}, device_id_type=MESH)
+        return carry
+
+    def greet_region(step, carry):
+        pl.semaphore_signal(barrier, inc=1, device_id={"region": lax.rem(region + step, 8)}, device_id_type=MESH)
+        return carry
+
+    lax.fori_loop(1, 16, greet_slab, 0)
+    lax.fori_loop(1, 8, greet_region, 0)
+    for t in range(11):
+        column = jnp.concatenate([coarse_ref[k, t] for k in range(4)], axis=0)
+        cols_send[t] = column.astype(BF)
+    pl.semaphore_wait(barrier, 22)
+
+    def copy_one(t, source, target):
+        return pltpu.make_async_remote_copy(
+            src_ref=cols_send.at[t],
+            dst_ref=cols_recv.at[source],
+            send_sem=send_one.at[t],
+            recv_sem=recv_one.at[source],
+            device_id={"slab": target},
+            device_id_type=MESH,
+        )
+
+    def start_one(t, carry):
+        target = lax.rem(11 * slab + t, 16)
+
+        @pl.when(target != slab)
+        def _():
+            copy_one(t, slab, target).start()
+
+        @pl.when(target == slab)
+        def _():
+            cols_recv[slab] = cols_send[t]
+
+        return carry
+
+    lax.fori_loop(0, 11, start_one, 0)
+
+    padded[pl.ds(0, 8), :] = jnp.zeros((8, 128), F32)
+    padded[pl.ds(8, 384), :] = up_ref[...]
+    padded[pl.ds(392, 8), :] = jnp.zeros((8, 128), F32)
+    for s in range(16):
+        hi, lo = split_hi_lo(padded[pl.ds(24 * s + 6, HALO), :])
+        weights[pl.ds(s * HALO, HALO), pl.ds(0, 128)] = hi
+        weights[pl.ds(s * HALO, HALO), pl.ds(128, 128)] = lo
+
+    def wait_one(source, carry):
+        t = lax.rem(slab + 5 * source, 16)
+
+        @pl.when((t < 11) & (source != slab))
+        def _():
+            copy_one(0, source, slab).wait_recv()
+
+        return carry
+
+    lax.fori_loop(0, 16, wait_one, 0)
+
+    def copy_two(target, source):
+        return pltpu.make_async_remote_copy(
+            src_ref=pick_send.at[target],
+            dst_ref=pick_recv.at[source],
+            send_sem=send_two.at[target],
+            recv_sem=recv_two.at[source],
+            device_id={"region": target},
+            device_id_type=MESH,
+        )
+
+    for r in range(8):
+        head = heads_ref[3 * r + 2]
+        place = lax.rem(slab - head + 176, 16)
+        wanted = lax.div(lax.rem(head + place, 176), 11)
+        pick_send[r] = cols_recv[wanted]
+
+        @pl.when(region != r)
+        def _():
+            copy_two(r, region).start()
+
+    pick_recv[region] = pick_send[region]
+
+    def wait_two(step, carry):
+        copy_two(0, lax.rem(region + step, 8)).wait_recv()
+        return carry
+
+    lax.fori_loop(1, 8, wait_two, 0)
+
+    first = heads_ref[3 * region] * 32 + heads_ref[3 * region + 1] * 8
+    row = lax.broadcasted_iota(jnp.int32, (128, 256), 0)
+    choose = (row + first == lax.broadcasted_iota(jnp.int32, (128, 256), 1)).astype(F32).astype(BF)
+    gathered = jnp.concatenate([pick_recv[b] for b in range(8)], axis=0)
+    patch = jnp.dot(choose, gathered, preferred_element_type=F32).astype(BF)
+    patch = jnp.concatenate([patch, patch], axis=0)
+
+    def copy_three(target, source):
+        return pltpu.make_async_remote_copy(
+            src_ref=rows_send.at[target],
+            dst_ref=rows_recv.at[source],
+            send_sem=send_three.at[target],
+            recv_sem=recv_three.at[source],
+            device_id={"slab": target},
+            device_id_type=MESH,
+        )
+
+    for part in range(4):
+        value = jnp.dot(weights[pl.ds(part * 128, 128), :], patch, preferred_element_type=F32)
+        for k in range(4):
+            s = part * 4 + k
+            rows_send[s] = value[k * HALO : (k + 1) * HALO].astype(BF)
+
+            @pl.when(slab != s)
+            def _():
+                copy_three(s, slab).start()
+
+    rows_recv[slab] = rows_send[slab]
+
+    def wait_three(step, carry):
+        copy_three(0, lax.rem(slab + step, 16)).wait_recv()
+        return carry
+
+    lax.fori_loop(1, 16, wait_three, 0)
+    out_ref[...] = rows_recv[...]
+
+    def done_one(t, carry):
+        @pl.when(lax.rem(11 * slab + t, 16) != slab)
+        def _():
+            copy_one(t, slab, slab).wait_send()
+
+        return carry
+
+    lax.fori_loop(0, 11, done_one, 0)
+
+    def done_two(step, carry):
+        copy_two(lax.rem(region + step, 8), region).wait_send()
+        return carry
+
+    lax.fori_loop(1, 8, done_two, 0)
+
+    def done_three(step, carry):
+        copy_three(lax.rem(slab + step, 16), slab).wait_send()
+        return carry
+
+    lax.fori_loop(1, 16, done_three, 0)
+
+
+def exchange(heads, coarse, up_rows):
+    vmem = pl.BlockSpec(memory_space=pltpu.VMEM)
+    return pl.pallas_call(
+        exchange_kernel,
+        out_shape=jax.ShapeDtypeStruct((16, HALO, 256), BF),
+        in_specs=[pl.BlockSpec(memory_space=pltpu.SMEM), vmem, vmem],
+        out_specs=vmem,
+        scratch_shapes=[
+            pltpu.VMEM((11, 32, 256), BF),
+            pltpu.VMEM((16, 32, 256), BF),
+            pltpu.VMEM((8, 32, 256), BF),
+            pltpu.VMEM((8, 32, 256), BF),
+            pltpu.VMEM((16, HALO, 256), BF),
+            pltpu.VMEM((16, HALO, 256), BF),
+            pltpu.VMEM((400, 128), F32),
+            pltpu.VMEM((512, 256), BF),
+            pltpu.SemaphoreType.DMA((11,)),
+            pltpu.SemaphoreType.DMA((16,)),
+            pltpu.SemaphoreType.DMA((8,)),
+            pltpu.SemaphoreType.DMA((8,)),
+            pltpu.SemaphoreType.DMA((16,)),
+            pltpu.SemaphoreType.DMA((16,)),
+        ],
+        compiler_params=pltpu.CompilerParams(collective_id=0, has_side_effects=True),
+        name="exchange",
+    )(heads, coarse, up_rows)
 
 
 def prepare_columns(cols_ref, split, uc):
@@ -110,19 +311,19 @@
     shifted,
     result,
 ):
-    start = sc_ref[0]
-    valid_rows = sc_ref[1]
-    valid_pairs = sc_ref[2]
-    first_row = sc_ref[3]
+    region = lax.axis_index("region")
+    valid_rows = sc_ref[24 + 2 * region] * 24
+    valid_pairs = sc_ref[25 + 2 * region] * 48
+    first_row = lax.axis_index("slab") * 24 - 2
 
     build_conv_weights(k1_ref, w1)
     build_conv_weights(k2_ref, w2)
     prepare_columns(cols_ref, split, uc)
     prepare_lift(lift_ref, lift_w)
     prepare_maps(class_ref, gain_ref, shift_ref, maps)
+    start = sc_ref[3 * region + 2]
     for place in range(16):
-        slot = lax.rem(place + start, 16)
-        block = rows_ref[slot]
+        block = rows_ref[lax.rem(place + start, 16)]
         block = jnp.concatenate([block, block], axis=1)
         value = jnp.dot(block, lift_w[...], preferred_element_type=F32)
         for w in range(4):
@@ -250,38 +451,11 @@
     gain_table,
     shift_table,
 ):
-    region = lax.axis_index("region")
     slab = lax.axis_index("slab")
-    columns = jnp.transpose(coarse.astype(BF), (1, 0, 2, 3)).reshape(11, 32, 256)
-    columns = jnp.concatenate([columns, jnp.zeros((5, 32, 256), BF)], axis=0)
-    columns = jnp.concatenate([columns, columns], axis=0)
-    columns = lax.dynamic_slice_in_dim(columns, lax.rem(5 * slab, 16), 16, 0)
-    columns = lax.all_to_all(columns, "slab", split_axis=0, concat_axis=0, tiled=True)
-    starts = cover[:, 0, 0, 2]
-    place = jnp.remainder(slab - starts, 16)
-    wanted = jnp.remainder(starts + place, 176) // 11
-    picked = columns[wanted]
-    mine = lax.all_to_all(picked, "region", split_axis=0, concat_axis=0, tiled=True)
-    first_block = cover[region, 0, 0, 0] * 4 + cover[region, 0, 0, 1]
-    patch = lax.dynamic_slice_in_dim(mine.reshape(256, 256), first_block * 8, 128, 0)
-    padded_rows = jnp.pad(up_rows, ((2, 6), (0, 0)))
-    rows_w = jnp.concatenate([padded_rows[24 * s : 24 * s + HALO] for s in range(16)], axis=0)
-    rows_hi = lax.reduce_precision(rows_w, 8, 7)
-    rows_w = jnp.concatenate([rows_hi.astype(BF), (rows_w - rows_hi).astype(BF)], axis=1)
-    up = jnp.dot(rows_w, jnp.concatenate([patch, patch], axis=0), preferred_element_type=F32)
-    up = up.astype(BF).reshape(16, HALO, 256)
-    up = lax.all_to_all(up, "slab", split_axis=0, concat_axis=0, tiled=True)
-
+    scalars = jnp.concatenate([cover[:, 0, 0, :].reshape(24), sizes.reshape(16)])
+    up = exchange(scalars, coarse, up_rows)
     tile_rows = jnp.clip(3 * slab - 1 + jnp.arange(8, dtype=jnp.int32), 0, 47)
     classes = tclass[0][tile_rows]
-    scalars = jnp.stack(
-        [
-            lax.rem(cover[region, 0, 0, 2], 16),
-            sizes[region, 0] * 24,
-            sizes[region, 1] * 48,
-            slab * 24 - 2,
-        ]
-    ).astype(jnp.int32)
     out = compute(scalars, up, lift, up_cols, kernel_one, kernel_two, classes, gain_table, shift_table)
     return out[None]
 

time: 93 us -> 70.6 us (0.76); the launches traced: 91.5 us -> 70.2 us
  Pallas kernels: 39.6 us -> 65.3 us
  starting transfers between devices: 19.7 us -> 0 us
  local copies, waits for them, and re-layouts: 18.7 us -> 4.26 us
  waiting for transfers between devices: 6.49 us -> 0 us
  between operations: 4.45 us -> 0.02 us
  other arithmetic: 1.64 us -> 0.63 us
  matrix products: 0.94 us -> 0 us
    pallas_call x0 -> x1, Pallas kernels: none -> 25.8 us  [exchange(): pl.pallas_call(exchange_kernel, out_shape=jax.ShapeDtypeStruct((16, HALO,...]
    all_to_all x3 -> x0, starting transfers between devices: 19.7 us -> none  [the longest x1 7.99 us: local(): lax.all_to_all(columns, 'slab', split_axis=0, concat_axis=0, tiled=True)]
    unnamed x22 -> x3, local copies, waits for them, and re-layouts: 12.7 us -> 1.55 us
    all_to_all x3 -> x0, waiting for transfers between devices: 6.49 us -> none  [the longest x1 3.47 us: local(): lax.all_to_all(picked, 'region', split_axis=0, concat_axis=0, tiled=True)]
    dynamic_slice x3 -> x0, local copies, waits for them, and re-layouts: 1.93 us -> none  [the longest x1 1.31 us: local(): first_block = cover[region, 0, 0, 0] * 4 + cover[region, 0, 0, 1]]
    gather x1 -> x0, local copies, waits for them, and re-layouts: 1.21 us -> none  [local(): picked = columns[wanted]]
    dot_general x1 -> x0, matrix products: 0.94 us -> none  [local(): jnp.dot(rows_w, jnp.concatenate([patch, patch], axis=0), preferred_elemen...]
  transfers between devices with their start and end apart: 3 -> 0, of which waited for: 2 -> 0; matrix products, arithmetic and copies ran while one was open for 18% -> 0% of each run, Pallas kernels for 0% -> 0%
where the time goes in v3:
time: 70.6 us; the launch traced here: 70.2 us
  Pallas kernels  65.3 us (92%)
  local copies, waits for them, and re-layouts  4.26 us (6%)
    pallas_call x1, Pallas kernels, compute(): pl.pallas_call(compute_kernel, out_shape=jax.ShapeDtypeStruct((ROWS, PAIR...  39.5 us
    pallas_call x1, Pallas kernels, exchange(): pl.pallas_call(exchange_kernel, out_shape=jax.ShapeDtypeStruct((16, HALO,...  25.8 us
    unnamed x3, local copies, waits for them, and re-layouts  1.55 us

profile of v3, /device:TPU:0, one launch (start us, length us, event | category | flops | bytes accessed | tf_op | source)
XLA Modules:
  0.0 70.2 jit_solution(13613358840545591131)
XLA Ops:
  0.0 0.0 copy-start
  0.0 0.8 %copy-done = s32[1,48,192]{2,1,0:T(8,128)S(1)} copy-done((s32[1,48,192]{2,1,0:T(8,128)S(1)}, s32[1,48,192]{2,1,0:T(8,128)}, u32[]{:S(2)}) %copy-start) | copy-done | bytes 36888
  0.8 1.1 %gather_fusion = s32[8,192]{1,0:T(8,128)} fusion(s32[48,192]{1,0:T(8,128)S(1)} %bitcast.4, s32[1024]{0:T(1024)S(1)} %pad_clamp_fusion), kind=kCustom, calls=%fused_computation | custom fusion | bytes 12320 | tf_op jit(solution)/shard_map/gather | solution.py:458
  2.0 1.4 %slice_reduce_fusion = s32[8,3]{1,0:T(8,128)S(1)} fusion(s32[8,16,16,3]{2,1,3,0:T(8,128)} %param.12), kind=kLoop, calls=%fused_computation.1 | loop fusion | bytes 192 | tf_op jit(solution)/shard_map/slice | solution.py:455
  3.4 0.1 reshape_squeeze.3
  3.4 0.8 %copy.13 = s32[8,2]{1,0:T(8,128)S(1)} copy(s32[8,2]{0,1:T(2,128)} %param.13) | data formatting | bytes 128 | tf_op args[2]
  4.2 0.1 reshape.22
  4.3 0.6 pad_add_fusion.heads_ref.sc_ref
  4.9 25.8 %exchange.1.rows_ref = bf16[16,32,256]{2,1,0:T(8,128)(2,1)} custom-call(s32[40]{0:T(128)} %pad_add_fusion.heads_ref.sc_ref, f32[4,11,8,256]{3,2,1,0:T(8,128)} %coarse_ref.1, f32[384,128]{1,0:T(8,128)} %up_ref.1), custom_call_target="tpu_custom_call" | custom-call | tf_op jit(solution)/shard_map/exchange/pallas_call | solution.py:219
  30.7 39.5 %block.1 = bf16[24,98304]{1,0:T(8,128)(2,1)} custom-call(s32[40]{0:T(128)} %pad_add_fusion.heads_ref.sc_ref, bf16[16,32,256]{2,1,0:T(8,128)(2,1)} %exchange.1.rows_ref, f32[32,64]{1,0:T(8,128)} %lift_ref.1, f32[128,1536]{1,0:T(8,128)} %cols_ref.1, bf16[3,3,64,64]{3,2,1,0:T(8,128)(2,1)} %k1_ref.1, bf16[3,3,64,64]{3,2,1,0:T(8,128)(2,1)} %k2_ref.1, ...), custom_call_target="tpu_custom_call" | custom-call | tf_op jit(solution)/shard_map/block/pallas_call | solution.py:417
  (2 shorter events, 0.0 us)
Async XLA Ops:
  0.0 0.8 %copy-start = (s32[1,48,192]{2,1,0:T(8,128)S(1)}, s32[1,48,192]{2,1,0:T(8,128)}, u32[]{:S(2)}) copy-start(s32[1,48,192]{2,1,0:T(8,128)} %param.14) | copy-start | bytes 110596

commit v4 on v3

--- a/solution.py
+++ b/solution.py
@@ -10,6 +10,10 @@
 ROWS = 24
 HALO = 32
 PAIRS = 768
+CHUNK = 128
+BAND = 256
+STRIDE = 776
+EMIT = 96
 
 
 def split_hi_lo(value):
@@ -242,11 +246,12 @@
     )(heads, coarse, up_rows)
 
 
-def prepare_columns(cols_ref, split, uc):
+def prepare_columns(cols_ref, valid_pairs, split, uc):
     source = lax.broadcasted_iota(jnp.int32, (256, 256), 0)
     target = lax.broadcasted_iota(jnp.int32, (256, 256), 1)
     chosen = jnp.where(target < 128, 2 * target, 2 * target - 255)
     select = (source == chosen).astype(F32).astype(BF)
+    pair = lax.broadcasted_iota(jnp.int32, (128, 256), 0)
     for chunk in range(6):
         halves = split_hi_lo(cols_ref[:, pl.ds(chunk * 256, 256)])
         for part in range(2):
@@ -259,6 +264,7 @@
                 for q, parity in ((0, 0), (1, 1), (1, 0), (0, 1)):
                     pieces.append(split[pl.ds(part * 256 + parity * 128 + 2 * w + q, 16, stride=8), :])
             block = jnp.concatenate(pieces, axis=0).T
+            block = jnp.where(pair + chunk * 128 < valid_pairs, block, 0.0)
             uc[pl.ds(chunk * 128, 128), pl.ds(part * 256, 256)] = block.astype(BF)
 
 
@@ -272,15 +278,18 @@
             lift_w[pl.ds(part * 256 + bw * 32, 32), pl.ds(bw // 2 * 128, 128)] = sides[bw % 2].astype(BF)
 
 
-def prepare_maps(class_ref, gain_ref, shift_ref, maps):
+def prepare_maps(class_ref, gain_ref, shift_ref, size_rows, slab, valid_pairs, maps):
     gain, shift = gain_ref[...], shift_ref[...]
     table = jnp.concatenate(split_hi_lo(jnp.concatenate([gain, gain, shift, shift], axis=1)), axis=0)
     owner = lax.broadcasted_iota(jnp.int32, (192, PAIRS), 1) // 4
-    widen = (owner == lax.broadcasted_iota(jnp.int32, (192, PAIRS), 0)).astype(F32).astype(BF)
+    inside = lax.broadcasted_iota(jnp.int32, (192, PAIRS), 1) < valid_pairs
+    widen = (inside & (owner == lax.broadcasted_iota(jnp.int32, (192, PAIRS), 0))).astype(F32).astype(BF)
     ids = lax.broadcasted_iota(jnp.int32, (32, 192), 0) % 16
     hots = []
     for tile_row in range(5):
-        hots.append((class_ref[pl.ds(tile_row, 1), :] == ids).astype(F32))
+        place = 3 * slab - 1 + tile_row
+        row_valid = (place >= 0) & (place < 3 * size_rows)
+        hots.append((row_valid & (class_ref[pl.ds(tile_row, 1), :] == ids)).astype(F32))
     wide = jnp.dot(jnp.concatenate(hots, axis=0).astype(BF), widen, preferred_element_type=F32)
     for tile_row in range(5):
         hot = wide[tile_row * 32 : (tile_row + 1) * 32].T.astype(BF)
@@ -308,44 +317,52 @@
     hid_in,
     fine,
     maps,
-    shifted,
+    act_out,
+    hid_out,
     result,
+    staged,
+    sems,
 ):
     region = lax.axis_index("region")
-    valid_rows = sc_ref[24 + 2 * region] * 24
+    slab = lax.axis_index("slab")
+    start = sc_ref[3 * region + 2]
+    size_rows = sc_ref[24 + 2 * region]
     valid_pairs = sc_ref[25 + 2 * region] * 48
-    first_row = lax.axis_index("slab") * 24 - 2
 
     build_conv_weights(k1_ref, w1)
     build_conv_weights(k2_ref, w2)
-    prepare_columns(cols_ref, split, uc)
+    prepare_columns(cols_ref, valid_pairs, split, uc)
     prepare_lift(lift_ref, lift_w)
-    prepare_maps(class_ref, gain_ref, shift_ref, maps)
-    start = sc_ref[3 * region + 2]
+    prepare_maps(class_ref, gain_ref, shift_ref, size_rows, slab, valid_pairs, maps)
+    row = slab * 24 - 2 + lax.broadcasted_iota(jnp.int32, (HALO, 128), 0)
+    row_valid = (row >= 0) & (row < size_rows * 24)
     for place in range(16):
         block = rows_ref[lax.rem(place + start, 16)]
         block = jnp.concatenate([block, block], axis=1)
         value = jnp.dot(block, lift_w[...], preferred_element_type=F32)
         for w in range(4):
-            lifted[pl.ds((w * 16 + place) * HALO, HALO), :] = value[:, w * 128 : (w + 1) * 128]
+            lifted[pl.ds((w * 16 + place) * HALO, HALO), :] = jnp.where(
+                row_valid, value[:, w * 128 : (w + 1) * 128], 0.0
+            )
 
     zeros8 = jnp.zeros((8, 128), F32)
-    for row in range(2):
-        shifted[row, pl.ds(0, 8), :] = zeros8
-        shifted[row, pl.ds(8 + PAIRS, 8), :] = zeros8
-    pair_ids = lax.broadcasted_iota(jnp.int32, (PAIRS, 128), 0)
-    lane_low = lax.broadcasted_iota(jnp.int32, (PAIRS, 128), 1) < 64
-    col_valid = pair_ids < valid_pairs
+    for buffer in (act_out, hid_out):
+        for row in range(2):
+            buffer[row, pl.ds(0, 8), :] = zeros8
+            buffer[row, pl.ds(8 + PAIRS, 8), :] = zeros8
+    low = lax.broadcasted_iota(jnp.int32, (CHUNK, 128), 1) < 64
     low16 = lax.broadcasted_iota(jnp.int32, (16, 128), 1) < 64
 
-    def spread(row, value, dst_ref, pair):
-        shifted[row, pl.ds(8, PAIRS), :] = value
-        after = shifted[row, pl.ds(9, PAIRS), :]
-        before = shifted[row, pl.ds(7, PAIRS), :]
-        dst_ref[pair, :, pl.ds(row * 256, 128)] = value.astype(BF)
-        dst_ref[pair, :, pl.ds(row * 256 + 128, 128)] = jnp.where(lane_low, after, before).astype(BF)
-
-    def stage_one(pair, carry):
+    def spread(src_ref, dst_ref, pair):
+        for row in range(2):
+            for c in range(0, PAIRS, CHUNK):
+                own = src_ref[row, pl.ds(8 + c, CHUNK), :]
+                after = src_ref[row, pl.ds(9 + c, CHUNK), :]
+                before = src_ref[row, pl.ds(7 + c, CHUNK), :]
+                dst_ref[pair, pl.ds(c, CHUNK), pl.ds(row * 256, 128)] = own.astype(BF)
+                dst_ref[pair, pl.ds(c, CHUNK), pl.ds(row * 256 + 128, 128)] = jnp.where(low, after, before).astype(BF)
+
+    def upsample(pair):
         sides = []
         for row in range(2):
             parts = []
@@ -360,56 +377,83 @@
                 ]
             side = jnp.concatenate(parts, axis=0).astype(BF)
             sides.append(jnp.concatenate([side, side], axis=0))
-        value = jnp.dot(uc[...], jnp.concatenate(sides, axis=1), preferred_element_type=F32)
-        for row in range(2):
-            global_row = first_row + pair * 2 + row
-            keep = col_valid & ((global_row >= 0) & (global_row < valid_rows))
-            rounded = jnp.where(keep, value[:, row * 128 : (row + 1) * 128], 0.0).astype(BF)
-            fine[pair, :, pl.ds(row * 128, 128)] = rounded
-            spread(row, silu(rounded.astype(F32)), act_in, pair)
-        return carry
-
-    lax.fori_loop(0, 14, stage_one, 0)
-
-    def conv(src_ref, pair, w_ref):
-        window = jnp.concatenate([src_ref[pair], src_ref[pair + 1]], axis=1)
+        side = jnp.concatenate(sides, axis=1)
+        for c in range(0, PAIRS, BAND):
+            value = jnp.dot(uc[pl.ds(c, BAND), :], side, preferred_element_type=F32)
+            for row in range(2):
+                rounded = value[:, row * 128 : (row + 1) * 128].astype(BF)
+                fine[pair, pl.ds(c, BAND), pl.ds(row * 128, 128)] = rounded
+                act_out[row, pl.ds(8 + c, BAND), :] = silu(rounded.astype(F32))
+
+    def conv(src_ref, pair, c, w_ref):
+        window = jnp.concatenate([src_ref[pair, pl.ds(c, BAND), :], src_ref[pair + 1, pl.ds(c, BAND), :]], axis=1)
         return jnp.dot(window, w_ref[...], preferred_element_type=F32)
 
-    def stage_two(pair, carry):
-        value = conv(act_in, pair, w1)
-        for row in range(2):
-            local_row = pair * 2 + row
-            tile_row = lax.div(local_row + 7, 8)
-            global_row = first_row + 1 + local_row
-            gain = maps[tile_row, :, pl.ds(0, 128)]
-            shift = maps[tile_row, :, pl.ds(128, 128)]
-            keep = col_valid & ((global_row >= 0) & (global_row < valid_rows))
-            moved = value[:, row * 128 : (row + 1) * 128] * gain + shift
-            spread(row, jnp.where(keep, silu(moved), 0.0), hid_in, pair)
-        return carry
-
-    lax.fori_loop(0, 13, stage_two, 0)
-
-    def stage_three(pair, carry):
-        value = conv(hid_in, pair, w2)
-        for row in range(2):
-            global_row = first_row + 2 + pair * 2 + row
-            keep = col_valid & (global_row < valid_rows)
-            total = fine[pair + 1, :, pl.ds(row * 128, 128)].astype(F32) + value[:, row * 128 : (row + 1) * 128]
-            at = pl.multiple_of((pair * 2 + row) * PAIRS, PAIRS)
-            result[pl.ds(at, PAIRS), :] = jnp.where(keep, total, 0.0)
-        return carry
-
-    lax.fori_loop(0, 12, stage_three, 0)
-
-    def emit(group, carry):
-        for k in range(16):
-            p = group * 16 + k
-            got = [result[pl.ds(p + 8 * r * PAIRS, 8, stride=PAIRS), :] for r in range(3)]
-            out_ref[:, pl.ds(pl.multiple_of(p * 128, 128), 128)] = jnp.concatenate(got, axis=0).astype(BF)
-        return carry
-
-    lax.fori_loop(0, PAIRS // 16, emit, 0)
+    def first_conv(pair):
+        for c in range(0, PAIRS, BAND):
+            value = conv(act_in, pair, c, w1)
+            for row in range(2):
+                tile_row = lax.div(pair * 2 + row + 7, 8)
+                gain = maps[tile_row, pl.ds(c, BAND), pl.ds(0, 128)]
+                shift = maps[tile_row, pl.ds(c, BAND), pl.ds(128, 128)]
+                hid_out[row, pl.ds(8 + c, BAND), :] = silu(value[:, row * 128 : (row + 1) * 128] * gain + shift)
+
+    def second_conv(pair):
+        for c in range(0, PAIRS, BAND):
+            value = conv(hid_in, pair, c, w2)
+            for row in range(2):
+                total = fine[pair + 1, pl.ds(c, BAND), pl.ds(row * 128, 128)].astype(F32)
+                at = pl.multiple_of((pair * 2 + row) * STRIDE + c, 8)
+                result[pl.ds(at, BAND), :] = total + value[:, row * 128 : (row + 1) * 128]
+
+    def steps(first, last, last_two=False, last_one=False, up=False, one=False, two=False):
+        def body(k, carry):
+            if two:
+                second_conv(k - 6)
+            if one or last_two:
+                spread(hid_out, hid_in, jnp.clip(k - 4, 0, 12))
+            if one:
+                first_conv(k - 3)
+            if up or last_one:
+                spread(act_out, act_in, jnp.clip(k - 1, 0, 13))
+            if up:
+                upsample(k)
+            return carry
+
+        lax.fori_loop(first, last, body, 0)
+
+    steps(0, 3, up=True)
+    steps(3, 6, up=True, one=True)
+    steps(6, 14, up=True, one=True, two=True)
+    steps(14, 16, last_one=True, one=True, two=True)
+    steps(16, 18, last_two=True, two=True)
+
+    shown = jnp.where(slab < size_rows, valid_pairs, 0)
+
+    def copy_out(chunk):
+        span = pl.ds(pl.multiple_of(chunk * (EMIT * 128), EMIT * 128), EMIT * 128)
+        return pltpu.make_async_copy(staged.at[:, span], out_ref.at[:, span], sems.at[chunk])
+
+    def emit(chunk, carry):
+        def inner(group, carry):
+            for k in range(16):
+                p = chunk * EMIT + group * 16 + k
+                got = [result[pl.ds(p + 8 * r * STRIDE, 8, stride=STRIDE), :] for r in range(3)]
+                value = jnp.where(p < shown, jnp.concatenate(got, axis=0), 0.0)
+                staged[:, pl.ds(pl.multiple_of(p * 128, 128), 128)] = value.astype(BF)
+            return carry
+
+        lax.fori_loop(0, EMIT // 16, inner, 0)
+        copy_out(chunk).start()
+        return carry
+
+    lax.fori_loop(0, PAIRS // EMIT, emit, 0)
+
+    def drain(chunk, carry):
+        copy_out(chunk).wait()
+        return carry
+
+    lax.fori_loop(0, PAIRS // EMIT, drain, 0)
 
 
 def compute(scalars, *operands):
@@ -418,7 +462,7 @@
         compute_kernel,
         out_shape=jax.ShapeDtypeStruct((ROWS, PAIRS * 128), BF),
         in_specs=[pl.BlockSpec(memory_space=pltpu.SMEM)] + [vmem] * len(operands),
-        out_specs=vmem,
+        out_specs=pl.BlockSpec(memory_space=pltpu.HBM),
         scratch_shapes=[
             pltpu.VMEM((1024, 256), BF),
             pltpu.VMEM((1024, 256), BF),
@@ -431,7 +475,10 @@
             pltpu.VMEM((14, PAIRS, 256), BF),
             pltpu.VMEM((5, PAIRS, 256), F32),
             pltpu.VMEM((2, PAIRS + 16, 128), F32),
-            pltpu.VMEM((ROWS * PAIRS, 128), F32),
+            pltpu.VMEM((2, PAIRS + 16, 128), F32),
+            pltpu.VMEM((ROWS * STRIDE, 128), F32),
+            pltpu.VMEM((ROWS, PAIRS * 128), BF),
+            pltpu.SemaphoreType.DMA((PAIRS // EMIT,)),
         ],
         compiler_params=pltpu.CompilerParams(vmem_limit_bytes=63 * 1024 * 1024),
         name="block",

time: 70.6 us -> 57.2 us (0.81)
  Pallas kernels: 65.3 us -> 51.9 us
    pallas_call x1, Pallas kernels: 39.5 us -> 26.1 us  [compute(): pl.pallas_call(compute_kernel, out_shape=jax.ShapeDtypeStruct((ROWS, PAIR...]
where the time goes in v4:
time: 57.2 us; the launch traced here: 56.8 us
  Pallas kernels  51.9 us (91%)
  local copies, waits for them, and re-layouts  4.26 us (7%)
  other arithmetic  0.63 us (1%)
    pallas_call x1, Pallas kernels, compute(): pl.pallas_call(compute_kernel, out_shape=jax.ShapeDtypeStruct((ROWS, PAIR...  26.1 us
    pallas_call x1, Pallas kernels, exchange(): pl.pallas_call(exchange_kernel, out_shape=jax.ShapeDtypeStruct((16, HALO,...  25.8 us
    unnamed x3, local copies, waits for them, and re-layouts  1.55 us
    slice x1, local copies, waits for them, and re-layouts, local(): cover[:, 0, 0, :].reshape(24)  1.4 us
    gather x1, local copies, waits for them, and re-layouts, local(): classes = tclass[0][tile_rows]  1.15 us

profile of v4, /device:TPU:0, one launch (start us, length us, event | category | flops | bytes accessed | tf_op | source)
XLA Modules:
  0.0 56.8 jit_solution(5946549950079874817)
XLA Ops:
  0.0 0.0 copy-start
  0.0 0.8 %copy-done = s32[1,48,192]{2,1,0:T(8,128)S(1)} copy-done((s32[1,48,192]{2,1,0:T(8,128)S(1)}, s32[1,48,192]{2,1,0:T(8,128)}, u32[]{:S(2)}) %copy-start) | copy-done | bytes 36888
  0.8 1.1 %gather_fusion = s32[8,192]{1,0:T(8,128)} fusion(s32[48,192]{1,0:T(8,128)S(1)} %bitcast.4, s32[1024]{0:T(1024)S(1)} %pad_clamp_fusion), kind=kCustom, calls=%fused_computation | custom fusion | bytes 12320 | tf_op jit(solution)/shard_map/gather | solution.py:505
  2.0 1.4 %slice_reduce_fusion = s32[8,3]{1,0:T(8,128)S(1)} fusion(s32[8,16,16,3]{2,1,3,0:T(8,128)} %param.12), kind=kLoop, calls=%fused_computation.1 | loop fusion | bytes 192 | tf_op jit(solution)/shard_map/slice | solution.py:502
  3.4 0.1 reshape_squeeze.3
  3.4 0.8 %copy.13 = s32[8,2]{1,0:T(8,128)S(1)} copy(s32[8,2]{0,1:T(2,128)} %param.13) | data formatting | bytes 128 | tf_op args[2]
  4.2 0.1 reshape.22
  4.3 0.6 %pad_add_fusion.heads_ref.sc_ref = s32[40]{0:T(128)} fusion(s32[16]{0:T(128)S(1)} %reshape.22, s32[24]{0:T(128)S(1)} %reshape_squeeze.3), kind=kLoop, calls=%fused_computation.5 | loop fusion | flops 40 | bytes 320 | tf_op jit(solution)/shard_map/concatenate | solution.py:502
  4.9 25.8 %exchange.1.rows_ref = bf16[16,32,256]{2,1,0:T(8,128)(2,1)} custom-call(s32[40]{0:T(128)} %pad_add_fusion.heads_ref.sc_ref, f32[4,11,8,256]{3,2,1,0:T(8,128)} %coarse_ref.1, f32[384,128]{1,0:T(8,128)} %up_ref.1), custom_call_target="tpu_custom_call" | custom-call | tf_op jit(solution)/shard_map/exchange/pallas_call | solution.py:223
  30.7 26.1 %block.1 = bf16[24,98304]{1,0:T(8,128)(2,1)} custom-call(s32[40]{0:T(128)} %pad_add_fusion.heads_ref.sc_ref, bf16[16,32,256]{2,1,0:T(8,128)(2,1)} %exchange.1.rows_ref, f32[32,64]{1,0:T(8,128)} %lift_ref.1, f32[128,1536]{1,0:T(8,128)} %cols_ref.1, bf16[3,3,64,64]{3,2,1,0:T(8,128)(2,1)} %k1_ref.1, bf16[3,3,64,64]{3,2,1,0:T(8,128)(2,1)} %k2_ref.1, ...), custom_call_target="tpu_custom_call" | custom-call | tf_op jit(solution)/shard_map/block/pallas_call | solution.py:461
  (2 shorter events, 0.0 us)
Async XLA Ops:
  0.0 0.8 %copy-start = (s32[1,48,192]{2,1,0:T(8,128)S(1)}, s32[1,48,192]{2,1,0:T(8,128)}, u32[]{:S(2)}) copy-start(s32[1,48,192]{2,1,0:T(8,128)} %param.14) | copy-start | bytes 110596

commit v5 on v4

--- a/solution.py
+++ b/solution.py
@@ -49,7 +49,7 @@
 
 
 def exchange_kernel(
-    heads_ref,
+    cover_ref,
     coarse_ref,
     up_ref,
     out_ref,
@@ -61,6 +61,8 @@
     rows_recv,
     padded,
     weights,
+    heads,
+    heads_sem,
     send_one,
     recv_one,
     send_two,
@@ -71,6 +73,8 @@
     region = lax.axis_index("region")
     slab = lax.axis_index("slab")
 
+    fetch = pltpu.make_async_copy(cover_ref.at[:, :, 0, :], heads, heads_sem)
+    fetch.start()
     barrier = pltpu.get_barrier_semaphore()
 
     def greet_slab(step, carry):
@@ -142,8 +146,9 @@
             device_id_type=MESH,
         )
 
+    fetch.wait()
     for r in range(8):
-        head = heads_ref[3 * r + 2]
+        head = heads[r, 2, 0]
         place = lax.rem(slab - head + 176, 16)
         wanted = lax.div(lax.rem(head + place, 176), 11)
         pick_send[r] = cols_recv[wanted]
@@ -160,7 +165,7 @@
 
     lax.fori_loop(1, 8, wait_two, 0)
 
-    first = heads_ref[3 * region] * 32 + heads_ref[3 * region + 1] * 8
+    first = heads[region, 0, 0] * 32 + heads[region, 1, 0] * 8
     row = lax.broadcasted_iota(jnp.int32, (128, 256), 0)
     choose = (row + first == lax.broadcasted_iota(jnp.int32, (128, 256), 1)).astype(F32).astype(BF)
     gathered = jnp.concatenate([pick_recv[b] for b in range(8)], axis=0)
@@ -194,7 +199,9 @@
         return carry
 
     lax.fori_loop(1, 16, wait_three, 0)
-    out_ref[...] = rows_recv[...]
+    start = heads[region, 2, 0]
+    for place in range(16):
+        out_ref[place] = rows_recv[lax.rem(place + start, 16)]
 
     def done_one(t, carry):
         @pl.when(lax.rem(11 * slab + t, 16) != slab)
@@ -218,12 +225,12 @@
     lax.fori_loop(1, 16, done_three, 0)
 
 
-def exchange(heads, coarse, up_rows):
+def exchange(cover, coarse, up_rows):
     vmem = pl.BlockSpec(memory_space=pltpu.VMEM)
     return pl.pallas_call(
         exchange_kernel,
         out_shape=jax.ShapeDtypeStruct((16, HALO, 256), BF),
-        in_specs=[pl.BlockSpec(memory_space=pltpu.SMEM), vmem, vmem],
+        in_specs=[pl.BlockSpec(memory_space=pltpu.HBM), vmem, vmem],
         out_specs=vmem,
         scratch_shapes=[
             pltpu.VMEM((11, 32, 256), BF),
@@ -234,6 +241,8 @@
             pltpu.VMEM((16, HALO, 256), BF),
             pltpu.VMEM((400, 128), F32),
             pltpu.VMEM((512, 256), BF),
+            pltpu.SMEM((8, 3, 16), jnp.int32),
+            pltpu.SemaphoreType.DMA,
             pltpu.SemaphoreType.DMA((11,)),
             pltpu.SemaphoreType.DMA((16,)),
             pltpu.SemaphoreType.DMA((8,)),
@@ -243,7 +252,7 @@
         ],
         compiler_params=pltpu.CompilerParams(collective_id=0, has_side_effects=True),
         name="exchange",
-    )(heads, coarse, up_rows)
+    )(cover, coarse, up_rows)
 
 
 def prepare_columns(cols_ref, valid_pairs, split, uc):
@@ -289,7 +298,8 @@
     for tile_row in range(5):
         place = 3 * slab - 1 + tile_row
         row_valid = (place >= 0) & (place < 3 * size_rows)
-        hots.append((row_valid & (class_ref[pl.ds(tile_row, 1), :] == ids)).astype(F32))
+        classes = class_ref[pl.ds(jnp.clip(place, 0, 47), 1), :]
+        hots.append((row_valid & (classes == ids)).astype(F32))
     wide = jnp.dot(jnp.concatenate(hots, axis=0).astype(BF), widen, preferred_element_type=F32)
     for tile_row in range(5):
         hot = wide[tile_row * 32 : (tile_row + 1) * 32].T.astype(BF)
@@ -325,9 +335,8 @@
 ):
     region = lax.axis_index("region")
     slab = lax.axis_index("slab")
-    start = sc_ref[3 * region + 2]
-    size_rows = sc_ref[24 + 2 * region]
-    valid_pairs = sc_ref[25 + 2 * region] * 48
+    size_rows = sc_ref[0, region]
+    valid_pairs = sc_ref[1, region] * 48
 
     build_conv_weights(k1_ref, w1)
     build_conv_weights(k2_ref, w2)
@@ -337,7 +346,7 @@
     row = slab * 24 - 2 + lax.broadcasted_iota(jnp.int32, (HALO, 128), 0)
     row_valid = (row >= 0) & (row < size_rows * 24)
     for place in range(16):
-        block = rows_ref[lax.rem(place + start, 16)]
+        block = rows_ref[place]
         block = jnp.concatenate([block, block], axis=1)
         value = jnp.dot(block, lift_w[...], preferred_element_type=F32)
         for w in range(4):
@@ -498,12 +507,8 @@
     gain_table,
     shift_table,
 ):
-    slab = lax.axis_index("slab")
-    scalars = jnp.concatenate([cover[:, 0, 0, :].reshape(24), sizes.reshape(16)])
-    up = exchange(scalars, coarse, up_rows)
-    tile_rows = jnp.clip(3 * slab - 1 + jnp.arange(8, dtype=jnp.int32), 0, 47)
-    classes = tclass[0][tile_rows]
-    out = compute(scalars, up, lift, up_cols, kernel_one, kernel_two, classes, gain_table, shift_table)
+    up = exchange(jnp.transpose(cover, (0, 3, 1, 2)), coarse, up_rows)
+    out = compute(sizes.T, up, lift, up_cols, kernel_one, kernel_two, tclass[0], gain_table, shift_table)
     return out[None]
 
 

time: 57.2 us -> 52.1 us (0.911)
  local copies, waits for them, and re-layouts: 4.26 us -> 0 us
  other arithmetic: 0.63 us -> 0 us
    unnamed x3 -> x0, local copies, waits for them, and re-layouts: 1.55 us -> none
    slice x1 -> x0, local copies, waits for them, and re-layouts: 1.4 us -> none  [local(): cover[:, 0, 0, :].reshape(24)]
    gather x1 -> x0, local copies, waits for them, and re-layouts: 1.15 us -> none  [local(): classes = tclass[0][tile_rows]]
    concatenate x1 -> x0, other arithmetic: 0.61 us -> none  [local(): jnp.concatenate([cover[:, 0, 0, :].reshape(24), sizes.reshape(16)])]
where the time goes in v5:
time: 52.1 us; the launch traced here: 51.9 us
  Pallas kernels  51.9 us (100%)
    pallas_call x1, Pallas kernels, compute(): pl.pallas_call(compute_kernel, out_shape=jax.ShapeDtypeStruct((ROWS, PAIR...  26.1 us
    pallas_call x1, Pallas kernels, exchange(): pl.pallas_call(exchange_kernel, out_shape=jax.ShapeDtypeStruct((16, HALO,...  25.7 us

profile of v5, /device:TPU:0, one launch (start us, length us, event | category | flops | bytes accessed | tf_op | source)
XLA Modules:
  0.0 51.9 jit_solution(11848621863498944903)
XLA Ops:
  0.0 25.7 %exchange.1.rows_ref = bf16[16,32,256]{2,1,0:T(8,128)(2,1)} custom-call(s32[8,3,16,16]{3,2,1,0:T(8,128)} %bitcast.4, f32[4,11,8,256]{3,2,1,0:T(8,128)} %coarse_ref.1, f32[384,128]{1,0:T(8,128)} %up_ref.1), custom_call_target="tpu_custom_call" | custom-call | tf_op jit(solution)/shard_map/exchange/pallas_call | solution.py:230
  25.7 26.1 %block.1 = bf16[24,98304]{1,0:T(8,128)(2,1)} custom-call(s32[2,8]{1,0:T(2,128)} %bitcast.6, bf16[16,32,256]{2,1,0:T(8,128)(2,1)} %exchange.1.rows_ref, f32[32,64]{1,0:T(8,128)} %lift_ref.1, f32[128,1536]{1,0:T(8,128)} %cols_ref.1, bf16[3,3,64,64]{3,2,1,0:T(8,128)(2,1)} %k1_ref.1, bf16[3,3,64,64]{3,2,1,0:T(8,128)(2,1)} %k2_ref.1, s32[48,192]{1,0:T(8,128)} %bitcast.5, ...), custom_call_target="tpu_custom_call" | custom-call | tf_op jit(solution)/shard_map/block/pallas_call | solution.py:470
